TPU v7x, 32 devices: a whole 2x2x4 slice. The times are simulated.
32 devices in a mesh: dp: 8 (over y, x, core), tensor: 4 (over z).
Axes of the slice: x: 2, y: 2, z: 4, core: 2. Of those that a mesh axis runs over, the one named last changes fastest.
Arguments:
- layer_input: bfloat16 [24576, 768], P(('dp', 'tensor')), may hold values from -6 to 6
- output_grad: bfloat16 [24576, 768], P(('dp', 'tensor')), may hold values from -6 to 6
- query_weight: bfloat16 [768, 768], P('dp', 'tensor'), may hold values from -0.21875 to 0.21875
- key_weight: bfloat16 [768, 768], P('dp', 'tensor'), may hold values from -0.21875 to 0.21875
- value_weight: bfloat16 [768, 768], P('dp', 'tensor'), may hold values from -0.21875 to 0.21875
- out_weight: bfloat16 [768, 768], P('tensor', 'dp'), may hold values from -0.21875 to 0.21875
- up_weight: bfloat16 [768, 3072], P('dp', 'tensor'), may hold values from -0.21875 to 0.21875
- down_weight: bfloat16 [3072, 768], P('tensor', 'dp'), may hold values from -0.109375 to 0.109375
- query_bias: bfloat16 [12, 64], P('tensor', 'dp'), may hold values from -3 to 3
- value_bias: bfloat16 [12, 64], P('tensor', 'dp'), may hold values from -3 to 3
- inner_gain: bfloat16 [12, 64], P('tensor', 'dp'), may hold values from 0.25 to 1.75
- out_bias: bfloat16 [12, 64], P(None, 'dp'), may hold values from -3 to 3
- up_bias: bfloat16 [48, 64], P('tensor', 'dp'), may hold values from -3 to 3
- hidden_gain: bfloat16 [48, 64], P('tensor', 'dp'), may hold values from 0.25 to 1.75
- down_bias: bfloat16 [12, 64], P(None, 'dp'), may hold values from -3 to 3
- first_gain: bfloat16 [12, 64], P(None, 'dp'), may hold values from 0.25 to 1.75
- second_gain: bfloat16 [12, 64], P(None, 'dp'), may hold values from 0.25 to 1.75
- head_offsets: int32 [12, 5], P('tensor'), may hold values from 0 to 11
Outputs:
- layer_output: bfloat16 [24576, 768], P(('dp', 'tensor'))
- input_grad: bfloat16 [24576, 768], P(('dp', 'tensor'))
- grad_query_weight: float32 [768, 768], P('dp', 'tensor')
- grad_key_weight: float32 [768, 768], P('dp', 'tensor')
- grad_value_weight: float32 [768, 768], P('dp', 'tensor')
- grad_out_weight: float32 [768, 768], P('tensor', 'dp')
- grad_up_weight: float32 [768, 3072], P('dp', 'tensor')
- grad_down_weight: float32 [3072, 768], P('tensor', 'dp')
- grad_query_bias: float32 [12, 64], P('tensor', 'dp')
- grad_value_bias: float32 [12, 64], P('tensor', 'dp')
- grad_inner_gain: float32 [12, 64], P('tensor', 'dp')
- grad_out_bias: float32 [12, 64], P(None, 'dp')
- grad_up_bias: float32 [48, 64], P('tensor', 'dp')
- grad_hidden_gain: float32 [48, 64], P('tensor', 'dp')
- grad_down_bias: float32 [12, 64], P(None, 'dp')
- grad_first_gain: float32 [12, 64], P(None, 'dp')
- grad_second_gain: float32 [12, 64], P(None, 'dp')
All inputs are finite; a program needn't handle non-finite values.
Results may differ from a plain program's by a relative error of at most 0.02.
Values may be sent and summed in bfloat16 or wider, within the bound.
No kernel may reach another device: no remote copies, remote signals or barrier semaphores. Data moves between devices by JAX's collectives and lax.ppermute only.
A program may use at most 384 MiB of HBM per device.

v0:
```python
from functools import partial

import jax
import jax.numpy as jnp
from jax import lax
from jax.experimental import pallas as pl
from jax.experimental.pallas import tpu as pltpu
from jax.sharding import PartitionSpec as P

HEADS = 12
HD = 64
D = 768
FF = 3072
PROMPT = 2048
CONT = 512
ROWS = 768
HALF = ROWS // 2
TILE = 256
BLOCK = 256
PAIRS = HEADS // 2
DILATIONS = (2, 4, 6, 12)
PERIOD = 12
EPS = 1e-05
HERE = pl.BlockSpec(memory_space=pl.ANY)
LOG2E = 1.4426950408889634
NEG = -1e30
BF = jnp.bfloat16
F32 = jnp.float32


def dot(a, b):
    return jnp.dot(a, b, preferred_element_type=F32)


def dot_t(a, b):
    return lax.dot_general(a, b, (((1,), (1,)), ((), ())), preferred_element_type=F32)


def stats(v):
    mu = jnp.mean(v, -1, keepdims=True)
    var = jnp.mean(v * v, -1, keepdims=True) - mu * mu
    return mu, lax.rsqrt(var + EPS)


def normalize(v):
    mu, inv = stats(v)
    return (v - mu) * inv, inv


def norm_back(e, hat, inv):
    return inv * (
        e - jnp.mean(e, -1, keepdims=True) - hat * jnp.mean(e * hat, -1, keepdims=True)
    )


QB, VB, IG, UB, HG, OB, DB, FG, SG, VECTOR_ROWS = 0, 4, 8, 12, 24, 36, 48, 60, 72, 84


def by_head(ref, row):
    n = ref.shape[0]
    return jnp.concatenate([ref[i : i + 1, row * HD : row * HD + D // n] for i in range(n)], 1)


def by_unit(ref, row, i):
    return ref[i : i + 1, row * HD : row * HD + FF // ref.shape[0]]


def replicated(ref, row):
    return ref[0:1, row * HD : row * HD + D]


def by_parity(transposed):
    shape = (ROWS, ROWS)
    row = lax.broadcasted_iota(jnp.int32, shape, int(transposed))
    token = lax.broadcasted_iota(jnp.int32, shape, 1 - int(transposed))
    return jnp.where(token == jnp.where(row < HALF, 2 * row, 2 * (row - HALF) + 1), 1.0, 0.0).astype(BF)


def sort_kernel(x_ref, o_ref):
    o_ref[...] = dot(by_parity(False), x_ref[...]).astype(BF)


def sort_rows(x):
    spec = pl.BlockSpec((ROWS, D), lambda i: (0, 0))
    return pl.pallas_call(
        sort_kernel,
        grid=(1,),
        in_specs=[spec],
        out_specs=spec,
        out_shape=jax.ShapeDtypeStruct((ROWS, D), BF),
        name="sort_rows",
    )(x)


def project_kernel(x_ref, vec_ref, w_ref, n_ref, o_ref):
    hat, _ = normalize(x_ref[...].astype(F32))
    normed = (hat * replicated(vec_ref, FG)).astype(BF)
    n_ref[...] = normed
    n = o_ref.shape[1]
    if n == 3 * D:
        queries = dot(normed, w_ref[:, :D]) + by_head(vec_ref, QB)
        o_ref[:, :D] = (queries.astype(BF).astype(F32) * 0.125).astype(BF)
    o_ref[:, n - 2 * D : n - D] = dot(normed, w_ref[:, n - 2 * D : n - D]).astype(BF)
    o_ref[:, n - D :] = (dot(normed, w_ref[:, n - D :]) + by_head(vec_ref, VB)).astype(BF)


def project(x, vec, w):
    n = w.shape[1]
    return pl.pallas_call(
        project_kernel,
        out_shape=(
            jax.ShapeDtypeStruct((ROWS, D), BF),
            jax.ShapeDtypeStruct((ROWS, n), BF),
        ),
        grid=(ROWS // TILE,),
        in_specs=[
            pl.BlockSpec((TILE, D), lambda i: (i, 0)),
            pl.BlockSpec(vec.shape, lambda i: (0, 0)),
            pl.BlockSpec((D, n), lambda i: (0, 0), pipeline_mode=pl.Buffered(1)),
        ],
        out_specs=(
            pl.BlockSpec((TILE, D), lambda i: (i, 0)),
            pl.BlockSpec((TILE, n), lambda i: (i, 0)),
        ),
        cost_estimate=pl.CostEstimate(
            flops=2 * ROWS * D * n, bytes_accessed=2 * D * n + 2 * ROWS * (2 * D + n), transcendentals=0
        ),
        name="project",
    )(x, vec, w)


def token_info(shard):
    r = lax.iota(jnp.int32, ROWS)
    n = shard * ROWS + jnp.where(r < HALF, 2 * r, 2 * (r - HALF) + 1)
    prompt = n < PROMPT
    first = (n >= PROMPT) & (n < PROMPT + CONT)
    second = n >= PROMPT + CONT
    pos = jnp.where(second, n - CONT, n)
    return prompt, first, second, pos


def query_columns(shard, offsets):
    prompt, first, second, pos = token_info(shard)
    c = lax.iota(jnp.int32, HD)
    kc = (c % PERIOD)[None, None, :]
    qc = (pos % PERIOD)[:, None, None]
    count = jnp.zeros((ROWS, HEADS, HD), F32)
    for i, r in enumerate(DILATIONS):
        o = (offsets[:, i + 1] % r)[None, :, None]
        count = count + ((qc % r == o) & (kc % r == o)).astype(F32)
    to_prompt = (c < 2 * PERIOD)[None, None, :]
    own = jnp.where(to_prompt, prompt[:, None, None], True)
    count = count + own.astype(F32)
    logm = jnp.where(count > 0, jnp.log(jnp.maximum(count, 1.0)), NEG)
    high = lax.reduce_precision(logm, 8, 7)
    is_high = ((c // PERIOD) % 2 == 0)[None, None, :]
    table = jnp.where(is_high, high, logm - high)
    cc = c[None, None, :]
    bar = jnp.where(
        ((cc == 48) & second[:, None, None]) | ((cc == 49) & first[:, None, None]), NEG, 0.0
    )
    cols = jnp.where(cc < 4 * PERIOD, table, bar)
    cols = cols.reshape(ROWS, PAIRS, 2, HD)[:, :, ::-1, :]
    return cols.reshape(ROWS, PAIRS * 2 * HD).astype(BF)


def key_columns(shard):
    prompt, first, second, pos = token_info(shard)
    c = lax.iota(jnp.int32, 2 * HD) % HD
    hit = (pos % PERIOD)[:, None] == (c % PERIOD)[None, :]
    cc = c[None, :]
    one = jnp.where(cc < 2 * PERIOD, hit & prompt[:, None], hit & ~prompt[:, None])
    one = jnp.where(cc < 4 * PERIOD, one, (cc >= 50) & (cc < 53))
    one = jnp.where(cc == 48, first[:, None], one)
    one = jnp.where(cc == 49, second[:, None], one)
    return one.astype(BF)


def half_mask(rows, hh):
    lane = lax.broadcasted_iota(jnp.int32, (rows, 2 * HD), 1)
    return lane < HD if hh == 0 else lane >= HD


def plan(s, t):
    if s == 0:
        first = [0, 0, 0] if t < 3 else [0, 128, 128]
        return [
            (
                [(128 * i, 128), (HALF + 128 * i, 128)],
                [(k, 128 * (i + 1) - k), (HALF + k, 128 * (i + 1) - k)],
                True,
            )
            for i, k in enumerate(first)
        ]
    if t == 3:
        n = 256 if s == 1 else HALF
        pieces = [([(0, HALF)], [(0, n)], False), ([(HALF, HALF)], [(HALF, n)], False)]
        if s == 1:
            pieces.append(([(0, 128), (HALF, 128)], [(256, 128), (HALF + 256, 128)], False))
        return pieces
    return [([(i, TILE)], [(0, ROWS)], False) for i in range(0, ROWS, TILE)]


def take(a, ranges):
    parts = [a[at : at + n] for at, n in ranges]
    return parts[0] if len(parts) == 1 else jnp.concatenate(parts, 0)


def causal(p, queries, keys):
    def token(ranges, shape, axis):
        (at, n), _ = ranges
        i = lax.broadcasted_iota(jnp.int32, shape, axis)
        return jnp.where(i < n, 2 * (at + i), 2 * (at + i - n) + 1)

    rows, cols = p.shape
    mask = token(queries, (rows, 1), 0) >= token(keys, (1, cols), 1)
    return jnp.where(mask, p, 0.0)


def variants(s, t, run):
    if s < 3:
        pl.when((t >= s) & (t < 3))(partial(run, plan(s, 2)))
    pl.when(t == 3)(partial(run, plan(s, 3)))


def attend_kernel(t_ref, q_ref, aq_ref, *refs):
    k_refs, v_refs, (ak_ref, o_ref, qq_ref, acc_ref, m_ref, qs_ref) = refs[:4], refs[4:8], refs[8:]
    t = t_ref[0]
    low = half_mask(ROWS, 0)
    lane = lax.broadcasted_iota(jnp.int32, (ROWS, 2 * HD), 1)

    def lanes(hh):
        return slice(hh * 2 * HD, (hh + 1) * 2 * HD)

    def keys(hh, s):
        one = jnp.ones((ROWS, 2 * HD), BF)
        if hh == 0:
            return jnp.where(low, k_refs[s][...], ak_ref[s]), jnp.where(low, v_refs[s][...], one)
        return jnp.where(low, ak_ref[s], k_refs[s][...]), jnp.where(low, one, v_refs[s][...])

    for hh in range(2):
        a, b = (q_ref[...], aq_ref[...]) if hh == 0 else (aq_ref[...], q_ref[...])
        q = jnp.where(low, a, b)
        qq_ref[:, lanes(hh)] = q
        k, _ = keys(hh, 0)
        top = dot(q * k, jnp.ones((2 * HD, 2 * HD), BF)).astype(BF)
        m_ref[hh] = top.astype(F32)
        qs_ref[:, lanes(hh)] = jnp.where(lane == (HD if hh == 0 else 0) + 50, -top, q)
    acc_ref[...] = jnp.zeros_like(acc_ref)

    def pieces(s, todo):
        for hh in range(2):
            k, v = keys(hh, s)
            for queries, kept, cut in todo:
                q = take(qs_ref[:, lanes(hh)], queries)
                p = jnp.exp(dot_t(q, take(k, kept)))
                if cut:
                    p = causal(p, queries, kept)
                out, at = dot(p.astype(BF), take(v, kept)), 0
                for start, n in queries:
                    acc_ref[hh, start : start + n] += out[at : at + n]
                    at += n

    for s in range(4):
        variants(s, t, partial(pieces, s))

    other = jnp.where(low, acc_ref[1], acc_ref[0])
    bad = jnp.sum(jnp.where(other < 1e30, 0.0, 1.0))

    @pl.when(bad > 0)
    def _():
        m_ref[...] = jnp.full(m_ref.shape, NEG, F32)
        acc_ref[...] = jnp.zeros_like(acc_ref)

        def block(hh, i, s):
            rows = pl.ds(pl.multiple_of(i * TILE, TILE), TILE)
            at = pl.ds(pl.multiple_of(hh * 2 * HD, 2 * HD), 2 * HD)
            my = (lane < HD) == (hh == 0)
            k = jnp.where(my, k_refs[s][...], ak_ref[s])
            v = jnp.where(my, v_refs[s][...], jnp.ones((ROWS, 2 * HD), BF))
            scores = dot_t(qq_ref[rows, at], k)
            if s == 0:
                r = i * TILE + lax.broadcasted_iota(jnp.int32, (TILE, 1), 0)
                c = lax.broadcasted_iota(jnp.int32, (1, ROWS), 1)
                r = jnp.where(r < HALF, 2 * r, 2 * (r - HALF) + 1)
                c = jnp.where(c < HALF, 2 * c, 2 * (c - HALF) + 1)
                scores = jnp.where(r >= c, scores, NEG)
            old = m_ref[hh, rows]
            top = jnp.maximum(old, jnp.max(scores, -1, keepdims=True))
            p = jnp.exp(scores - top[:, :1])
            acc_ref[hh, rows] = acc_ref[hh, rows] * jnp.exp(old - top) + dot(p.astype(BF), v)
            m_ref[hh, rows] = top

        for s in range(4):

            @pl.when(t >= s)
            def _(s=s):
                def step(i, c):
                    block(i // 3, i % 3, s)
                    return c

                lax.fori_loop(0, 2 * ROWS // TILE, step, 0)

    a0, a1 = acc_ref[0], acc_ref[1]
    other = jnp.where(low, a1, a0)
    o_ref[...] = jnp.where(low, a0, a1) / pltpu.roll(other, HD, 1)
    lse = -(jnp.where(low, m_ref[1], m_ref[0]) + jnp.log(other))
    hi = lse.astype(BF)
    rest = lse - hi.astype(F32)
    mid = rest.astype(BF)
    lo = (rest - mid.astype(F32)).astype(BF)
    for hh in range(2):
        full = qq_ref[:, lanes(hh)]
        for j, piece in enumerate((hi, mid, lo)):
            full = jnp.where(lane == (HD if hh == 0 else 0) + 50 + j, piece, full)
        qq_ref[:, lanes(hh)] = full


def attend(t, own, others, aq, ak):
    pair = (ROWS, 2 * HD)

    def at(k):
        return pl.BlockSpec(pair, lambda p, t: (0, p + k))

    return pl.pallas_call(
        attend_kernel,
        grid_spec=pltpu.PrefetchScalarGridSpec(
            num_scalar_prefetch=1,
            grid=(PAIRS,),
            in_specs=[at(0), at(0)]
            + [at(PAIRS)] + [at(0)] * 3
            + [at(2 * PAIRS)] + [at(PAIRS)] * 3
            + [pl.BlockSpec((4, ROWS, 2 * HD), lambda p, t: (0, 0, 0))],
            out_specs=(at(0), pl.BlockSpec((ROWS, 4 * HD), lambda p, t: (0, p))),
            scratch_shapes=[
                pltpu.VMEM((2, ROWS, 2 * HD), F32),
                pltpu.VMEM((2, ROWS, 2 * HD), F32),
                pltpu.VMEM((ROWS, 4 * HD), BF),
            ],
        ),
        out_shape=(
            jax.ShapeDtypeStruct((ROWS, D), F32),
            jax.ShapeDtypeStruct((ROWS, 2 * D), BF),
        ),
        cost_estimate=pl.CostEstimate(
            flops=16 * 10**9, bytes_accessed=16 * 2**20, transcendentals=HEADS * ROWS * 2048
        ),
        name="attend",
    )(t, own, aq, own, *others, own, *others, ak)


def attend_back_kernel(own, s, t_ref, qq_ref, do_ref, k_ref, v_ref, ak_ref, dq_in_ref, w_ref, x_ref, *rest):
    dq_ref, dk_ref, dv_ref, dx_ref, sums_ref, dk_acc, dv_acc, keep_ref, dq_acc = rest
    p_id = pl.program_id(0)
    t = t_ref[0]
    last = PAIRS - 1

    low = half_mask(ROWS, 0)

    def work(todo):
        dk_acc[...] = jnp.zeros_like(dk_acc)
        dv_acc[...] = jnp.zeros_like(dv_acc)
        dq_acc[...] = jnp.zeros_like(dq_acc)
        one = jnp.ones((ROWS, 2 * HD), BF)
        for hh in range(2):
            lanes = slice(hh * 2 * HD, (hh + 1) * 2 * HD)
            half = slice(hh * HD, (hh + 1) * HD)
            if hh == 0:
                k, v = jnp.where(low, k_ref[...], ak_ref[0]), jnp.where(low, v_ref[...], one)
            else:
                k, v = jnp.where(low, ak_ref[0], k_ref[...]), jnp.where(low, one, v_ref[...])
            for queries, kept, cut in todo:
                q = take(qq_ref[:, lanes], queries)
                g = take(do_ref[:, lanes], queries)
                kk = take(k, kept)
                p = jnp.exp(dot_t(q, kk))
                if cut:
                    p = causal(p, queries, kept)
                ds = p * dot_t(g, take(v, kept))
                pb = p.astype(BF)
                sb = ds.astype(BF)
                part, at = dot(sb, kk), 0
                for start, n in queries:
                    dq_acc[hh, start : start + n] += part[at : at + n]
                    at += n
                dk = dot(q.astype(F32).T[half].astype(BF), sb)
                dv = dot(g.astype(F32).T[half].astype(BF), pb)
                at = 0
                for start, n in kept:
                    dk_acc[half, start : start + n] += dk[:, at : at + n]
                    dv_acc[half, start : start + n] += dv[:, at : at + n]
                    at += n
        dq = jnp.where(low, dq_acc[0], dq_acc[1]) * 0.125
        if dq_in_ref is not None:
            dq = dq_in_ref[...] + dq
        dq_ref[...] = dq.astype(dq_ref.dtype)
        dk = dk_acc[...].T.astype(BF)
        dv = dv_acc[...].T.astype(BF)
        keep_ref[p_id, :, : 2 * HD] = dk
        keep_ref[p_id, :, 2 * HD : 4 * HD] = dv
        if own:
            keep_ref[p_id, :, 4 * HD :] = dq.astype(BF)
        dk_ref[...] = dk
        dv_ref[...] = dv

        @pl.when(p_id == last)
        def _():
            def together(j):
                lanes = slice(j * 2 * HD, (j + 1) * 2 * HD)
                return jnp.concatenate([keep_ref[p, :, lanes] for p in range(PAIRS)], 1)

            wk = D if own else 0
            dvs = together(1)
            dx = dot_t(together(0), w_ref[:, wk : wk + D]) + dot_t(dvs, w_ref[:, wk + D :])
            sums_ref[...] = jnp.zeros_like(sums_ref)
            if own:
                dqs = together(2)
                dx += dot_t(dqs, w_ref[:, :D])
                sums_ref[0:1] = jnp.sum(dqs.astype(F32), 0, keepdims=True)
            sums_ref[1:2] = jnp.sum(dvs.astype(F32), 0, keepdims=True)
            hat, _ = normalize(x_ref[...].astype(F32))
            sums_ref[2:3] = jnp.sum(dx * hat, 0, keepdims=True)
            dx_ref[...] = dx.astype(dx_ref.dtype)

    variants(s, t, work)
    if not own:

        @pl.when(t < s)
        def _():
            dq_ref[...] = jnp.zeros_like(dq_ref) if dq_in_ref is None else dq_in_ref[...]
            dk_ref[...] = jnp.zeros_like(dk_ref)
            dv_ref[...] = jnp.zeros_like(dv_ref)
            dx_ref[...] = jnp.zeros_like(dx_ref)
            sums_ref[...] = jnp.zeros_like(sums_ref)


def attend_back(t, s, qq, wide, kv, ak, dq_in, w, x, first=()):
    pair = (ROWS, 2 * HD)
    own = s == 0
    k0 = PAIRS if own else 0

    def at(k):
        return pl.BlockSpec(pair, lambda p, t: (0, p + k))

    def used(p, t):
        return jnp.where(t[0] >= s, p, 0)

    def read(k, n=2):
        return pl.BlockSpec((ROWS, n * HD), lambda p, t: (0, used(p, t) + k))

    kernel = partial(attend_back_kernel, own, s)
    args = [t, qq, wide, kv, kv, ak]
    specs = [read(0, 4), read(0, 4), read(k0), read(k0 + PAIRS), pl.BlockSpec((1, ROWS, 2 * HD), lambda p, t: (s, 0, 0))]
    inner, n_first = kernel, len(first)
    n_in = 8 if dq_in is None else 9

    def kernel(*r):
        r = r[:n_in] + r[n_in + n_first :]
        return inner(*r) if dq_in is not None else inner(*r[:6], None, *r[6:])

    if dq_in is not None:
        args.append(dq_in)
        specs.append(at(0))
    args += [w, x, *first]
    specs += [
        pl.BlockSpec(w.shape, lambda p, t: (0, 0), pipeline_mode=pl.Buffered(1)),
        pl.BlockSpec((ROWS, D), lambda p, t: (0, 0), pipeline_mode=pl.Buffered(1)),
    ] + [HERE] * n_first
    return pl.pallas_call(
        kernel,
        grid_spec=pltpu.PrefetchScalarGridSpec(
            num_scalar_prefetch=1,
            grid=(PAIRS,),
            in_specs=specs,
            out_specs=(
                at(0), at(0), at(0),
                pl.BlockSpec((ROWS, D), lambda p, t: (0, 0)),
                pl.BlockSpec((8, D), lambda p, t: (0, 0)),
            ),
            scratch_shapes=[
                pltpu.VMEM((2 * HD, ROWS), F32),
                pltpu.VMEM((2 * HD, ROWS), F32),
                pltpu.VMEM((PAIRS, ROWS, 6 * HD), BF),
                pltpu.VMEM((2, ROWS, 2 * HD), F32),
            ],
        ),
        out_shape=(
            jax.ShapeDtypeStruct((ROWS, D), BF if own else F32),
            jax.ShapeDtypeStruct((ROWS, D), BF),
            jax.ShapeDtypeStruct((ROWS, D), BF),
            jax.ShapeDtypeStruct((ROWS, D), F32 if own else BF),
            jax.ShapeDtypeStruct((8, D), F32),
        ),
        cost_estimate=pl.CostEstimate(
            flops=16 * 10**9, bytes_accessed=16 * 2**20, transcendentals=HEADS * ROWS * ROWS
        ),
        name="attend_back",
    )(*args)


def normal_parts(v):
    e = jnp.exp2(v * v * (-0.5 * LOG2E))
    k = 1.0 / (1.0 + 0.2316419 * jnp.abs(v))
    p = 1.330274429 * k - 1.821255978
    for c in (1.781477937, -0.356563782, 0.319381530):
        p = p * k + c
    density = e * 0.3989422804014327
    tail = density * (p * k)
    return jnp.where(v >= 0, 1.0 - tail, tail), density


def middle_kernel(
    nt, c_ref, x_ref, g_ref, wo_ref, up_ref, down_ref, vec_ref,
    out_ref, n2_ref, hn_ref, pg_ref, inner_ref, bg_ref, mg_ref, wide_ref, sd_ref, sf_ref,
    act_ref, slope_ref, hgrad_ref,
):
    f = FF // nt

    def up_block(i):
        return up_ref[:, i].reshape(D, f)

    def down_block(i):
        return down_ref[:, i].reshape(D, f)

    @pl.when(pl.program_id(0) == 0)
    def _():
        sd_ref[...] = jnp.zeros_like(sd_ref)
        sf_ref[...] = jnp.zeros_like(sf_ref)

    def column(ref, row, lanes, v):
        ref[row : row + 1, lanes] += jnp.sum(v, 0, keepdims=True)

    every = slice(None)
    ig, ob, db, sg = by_head(vec_ref, IG), *(replicated(vec_ref, r) for r in (OB, DB, SG))
    context = c_ref[...]
    ch, cinv = normalize(context)
    inner = (ch * ig).astype(BF)
    inner_ref[...] = inner
    middle = x_ref[...].astype(F32) + (dot_t(inner, wo_ref[...]) + ob)
    sh, sinv = normalize(middle)
    n2 = (sh * sg).astype(BF)
    n2_ref[...] = n2
    g = g_ref[...]
    s1 = jnp.zeros((BLOCK, 1), F32)
    s2 = jnp.zeros((BLOCK, 1), F32)
    for i in range(nt):
        lanes = slice(i * f, (i + 1) * f)
        pre = dot(n2, up_block(i)) + by_unit(vec_ref, UB, i)
        phi, density = normal_parts(pre)
        act = pre * phi
        act_ref[:, lanes] = act
        slope_ref[:, lanes] = phi + pre * density
        hgrad_ref[:, lanes] = dot(g, down_block(i))
        s1 += jnp.sum(act, -1, keepdims=True)
        s2 += jnp.sum(act * act, -1, keepdims=True)
    mu = s1 / FF
    inv = lax.rsqrt(s2 / FF - mu * mu + EPS)
    e1 = jnp.zeros((BLOCK, 1), F32)
    e2 = jnp.zeros((BLOCK, 1), F32)
    branch = jnp.zeros((BLOCK, D), F32)
    for i in range(nt):
        lanes = slice(i * f, (i + 1) * f)
        hat = (act_ref[:, lanes] - mu) * inv
        act_ref[:, lanes] = hat
        hg = by_unit(vec_ref, HG, i)
        hn = (hat * hg).astype(BF)
        hn_ref[:, lanes] = hn
        branch += dot_t(hn, down_block(i))
        grad = hgrad_ref[:, lanes]
        gh = grad * hat
        column(sf_ref, 1, lanes, gh)
        e = grad * hg
        hgrad_ref[:, lanes] = e
        e1 += jnp.sum(e, -1, keepdims=True)
        e2 += jnp.sum(gh * hg, -1, keepdims=True)
    out_ref[...] = (middle + (branch + db)).astype(BF)
    e1 = e1 / FF
    e2 = e2 / FF
    back = jnp.zeros((BLOCK, D), F32)
    for i in range(nt):
        lanes = slice(i * f, (i + 1) * f)
        ag = inv * (hgrad_ref[:, lanes] - e1 - act_ref[:, lanes] * e2)
        pg = (ag * slope_ref[:, lanes]).astype(BF)
        pg_ref[:, lanes] = pg
        column(sf_ref, 0, lanes, pg.astype(F32))
        back += dot_t(pg, up_block(i))
    column(sd_ref, 0, every, back * sh)
    gf = g.astype(F32)
    mg = gf + norm_back(back * sg, sh, sinv)
    mg_ref[...] = mg
    bg = mg.astype(BF)
    bg_ref[...] = bg
    column(sd_ref, 1, every, bg.astype(F32))
    column(sd_ref, 2, every, gf)
    ingrad = dot(bg, wo_ref[...])
    column(sd_ref, 3, every, ingrad * ch)
    cg = norm_back(ingrad * ig, ch, cinv).astype(BF).astype(F32)
    lane = lax.broadcasted_iota(jnp.int32, (BLOCK, 2 * HD), 1)
    for p in range(PAIRS):
        pair = slice(p * 2 * HD, (p + 1) * 2 * HD)
        gp = cg[:, pair]
        prod = gp * context[:, pair]
        for hh in range(2):
            mine = half_mask(BLOCK, hh)
            d = -jnp.sum(jnp.where(mine, prod, 0.0), -1, keepdims=True)
            hi = d.astype(BF).astype(F32)
            mid = (d - hi).astype(BF).astype(F32)
            lo = d - hi - mid
            base = HD if hh == 0 else 0
            full = jnp.where(mine, gp, 0.0)
            full = jnp.where(lane == base, hi, full)
            full = jnp.where(lane == base + 1, mid, full)
            full = jnp.where(lane == base + 2, lo, full)
            at = (2 * p + hh) * 2 * HD
            wide_ref[:, at : at + 2 * HD] = full.astype(BF)


def middle_layer(nt, context, x, g, wo, ffn, vec):
    def rows(n):
        return pl.BlockSpec((BLOCK, n), lambda i: (i, 0))

    def whole(*shape):
        return pl.BlockSpec(shape, lambda i: (0,) * len(shape), pipeline_mode=pl.Buffered(1))

    def shape(n, kind):
        return jax.ShapeDtypeStruct((ROWS, n), kind)

    nb, _, _, r, f = ffn.shape

    def weight(j):
        return pl.BlockSpec(
            (nb, nt, None, r, f), lambda i: (0, 0, j, 0, 0), pipeline_mode=pl.Buffered(1)
        )

    return pl.pallas_call(
        partial(middle_kernel, nt),
        grid=(ROWS // BLOCK,),
        in_specs=[
            rows(D), rows(D), rows(D), whole(D, D), weight(0), weight(1), whole(*vec.shape),
        ],
        out_specs=(
            rows(D), rows(D), rows(FF), rows(FF), rows(D), rows(D), rows(D), rows(2 * D),
            pl.BlockSpec((8, D), lambda i: (0, 0)), pl.BlockSpec((8, FF), lambda i: (0, 0)),
        ),
        out_shape=(
            shape(D, BF), shape(D, BF), shape(FF, BF), shape(FF, BF), shape(D, BF), shape(D, BF),
            shape(D, F32), shape(2 * D, BF),
            jax.ShapeDtypeStruct((8, D), F32), jax.ShapeDtypeStruct((8, FF), F32),
        ),
        scratch_shapes=[pltpu.VMEM((BLOCK, FF), F32)] * 3,
        cost_estimate=pl.CostEstimate(
            flops=2 * ROWS * D * (4 * FF + 2 * D), bytes_accessed=30 * 2**20, transcendentals=ROWS * FF
        ),
        name="middle",
    )(context, x, g, wo, ffn, ffn, vec)


def tn(a, b):
    return lax.dot_general(a, b, (((0,), (0,)), ((), ())), preferred_element_type=F32)


def put(core, out_refs, value):
    shape = out_refs[0].shape
    if len(out_refs) == 1:
        out_refs[0][...] = value.astype(BF).reshape(shape)
        return
    value = value.astype(BF).reshape(shape[0], 2, *shape[1:])
    for i in range(2):

        @pl.when(core == i)
        def _(i=i):
            out_refs[0][...] = value[:, i]
            out_refs[1][...] = value[:, 1 - i]


def ffn_outer_kernel(core_ref, n2_ref, pg_ref, g_ref, hn_ref, *out_refs):
    @pl.when(pl.program_id(0) == 0)
    def _():
        put(core_ref[0], out_refs, tn(n2_ref[...], pg_ref[...]))

    @pl.when(pl.program_id(0) == 1)
    def _():
        put(core_ref[0], out_refs, tn(g_ref[...], hn_ref[...]))


def ffn_outer(core, nt, nb, outs, n2, pg, g, hn):
    f, r = FF // nt, D // nb
    left = pl.BlockSpec((ROWS, D), lambda j, i, c: (0, 0))
    return pl.pallas_call(
        ffn_outer_kernel,
        grid_spec=pltpu.PrefetchScalarGridSpec(
            num_scalar_prefetch=1,
            grid=(2, nt),
            in_specs=[
                left,
                pl.BlockSpec((ROWS, f), lambda j, i, c: (0, i * (1 - j) + (nt - 1) * j)),
                left,
                pl.BlockSpec((ROWS, f), lambda j, i, c: (0, i * j)),
            ],
            out_specs=(pl.BlockSpec((nb // outs, None, None, r, f), lambda j, i, c: (0, i, j, 0, 0)),) * outs,
        ),
        out_shape=(jax.ShapeDtypeStruct((nb // outs, nt, 2, r, f), BF),) * outs,
        cost_estimate=pl.CostEstimate(
            flops=4 * ROWS * D * FF, bytes_accessed=4 * D * FF + 4 * ROWS * FF, transcendentals=0
        ),
        name="ffn_outer",
    )(core, n2, pg, g, hn)


def attn_outer_kernel(terms, core_ref, ins, outs):
    for m, pairs in enumerate(terms):

        @pl.when(pl.program_id(0) == m)
        def _(pairs=pairs):
            total = tn(ins[pairs[0][0]][...], ins[pairs[0][1]][...])
            for a, b in pairs[1:]:
                total += tn(ins[a][...], ins[b][...])
            put(core_ref[0], outs, total)


def attn_outer(core, nb, outs, matrices, first):
    args = []
    for m in matrices:
        for pair in m:
            args += [v for v in pair if all(v is not w for w in args)]
    where = {id(v): i for i, v in enumerate(args)}
    terms = [[(where[id(u)], where[id(v)]) for u, v in m] for m in matrices]
    n = len(args)

    def kernel(core_ref, *refs):
        attn_outer_kernel(terms, core_ref, refs[:n], refs[n + len(first) :])

    r = D // nb
    whole = pl.BlockSpec((ROWS, D), lambda i, c: (0, 0), pipeline_mode=pl.Buffered(1))
    pairs = sum(len(m) for m in matrices)
    return pl.pallas_call(
        kernel,
        grid_spec=pltpu.PrefetchScalarGridSpec(
            num_scalar_prefetch=1,
            grid=(len(matrices),),
            in_specs=[whole] * n + [HERE] * len(first),
            out_specs=(pl.BlockSpec((nb // outs, r, D), lambda i, c: (0, 0, i)),) * outs,
        ),
        out_shape=(jax.ShapeDtypeStruct((nb // outs, r, len(matrices) * D), BF),) * outs,
        cost_estimate=pl.CostEstimate(
            flops=2 * pairs * ROWS * D * D, bytes_accessed=2 * n * ROWS * D, transcendentals=0
        ),
        name="attn_outer",
    )(core, *args, *first)


def halve_kernel(order_ref, *refs):
    ins, outs = refs[: len(refs) - 4], refs[-4:]
    for o in range(4):
        j = order_ref[o]
        total = ins[0][j].astype(F32) + ins[1][j].astype(F32)
        n = total.shape[-2]
        if len(ins) == 2:
            outs[o][...] = total.astype(BF)
        else:
            outs[o][:n] = total.astype(BF)
            outs[o][n:] = (ins[2][j].astype(F32) + ins[3][j].astype(F32)).astype(BF)


def halve(order, keep, got, small=None):
    if small is None:
        shape = keep.shape[1:]
        grid = (shape[0],)
        block = pl.BlockSpec((4, None, *shape[1:]), lambda i, o: (0, i, 0, 0, 0))
        out = pl.BlockSpec((None, *shape[1:]), lambda i, o: (i, 0, 0, 0))
        args, specs = [keep, got], [block] * 2
    else:
        n = 2
        rows, cols = keep.shape[1] + (small[0].shape[1] if small else 0), keep.shape[2]
        shape, grid = (rows, cols), (n,)

        def block(a):
            return pl.BlockSpec((4, a.shape[1], cols // n), lambda i, o: (0, 0, i))

        out = pl.BlockSpec((rows, cols // n), lambda i, o: (0, i))
        args = [keep, got, *small]
        specs = [block(a) for a in args]
    return pl.pallas_call(
        halve_kernel,
        grid_spec=pltpu.PrefetchScalarGridSpec(
            num_scalar_prefetch=1, grid=grid, in_specs=specs, out_specs=(out,) * 4
        ),
        out_shape=(jax.ShapeDtypeStruct(shape, BF),) * 4,
        cost_estimate=pl.CostEstimate(flops=keep.size, bytes_accessed=6 * keep.size, transcendentals=0),
        name="halve",
    )(order, *args)


def chips_kernel(cut, t_ref, *refs):
    ins, outs = refs[:4], refs[4:]
    nt = len(outs)
    if cut is None:
        for s in range(nt):
            j = lax.rem(t_ref[0] + s, nt)
            total = ins[0][j].astype(F32)
            for r in ins[1:]:
                total += r[j].astype(F32)
            outs[s][...] = total.astype(BF)
        return
    rows, cols = cut
    total = ins[0][...].astype(F32)
    for r in ins[1:]:
        total += r[...].astype(F32)
    total = total.astype(BF)
    blocks = []
    n = total.shape[1] // D
    for j in range(nt):
        at = [total[:rows, m * D + j * cols : m * D + (j + 1) * cols] for m in range(n)]
        block = [jnp.concatenate(at, 1)]
        if total.shape[0] > rows:
            left = (j % 2) * D
            block += [total[rows:, left + i * n * cols : left + (i + 1) * n * cols] for i in range(2)]
        blocks.append(jnp.concatenate(block, 0))
    for j in range(nt):

        @pl.when(t_ref[0] == j)
        def _(j=j):
            for s in range(nt):
                outs[s][...] = blocks[(j + s) % nt]


def chips(tvec, nt, parts, cut=None, first=()):
    shape = parts[0].shape[1:]
    if cut is not None:
        shape = (2 * parts[0].shape[0] - cut[0], parts[0].shape[1] // nt)
    n = len(parts)

    def kernel(t_ref, *refs):
        chips_kernel(cut, t_ref, *refs[:n], *refs[n + len(first) :])

    return pl.pallas_call(
        kernel,
        grid_spec=pltpu.PrefetchScalarGridSpec(
            num_scalar_prefetch=1,
            grid=(1,),
            in_specs=[pl.BlockSpec(p.shape, lambda i, t, n=p.ndim: (0,) * n) for p in parts] + [HERE] * len(first),
            out_specs=(pl.BlockSpec(shape, lambda i, t: (0,) * len(shape)),) * nt,
        ),
        out_shape=(jax.ShapeDtypeStruct(shape, BF),) * nt,
        cost_estimate=pl.CostEstimate(
            flops=4 * parts[0].size, bytes_accessed=10 * parts[0].size, transcendentals=0
        ),
        name="chips",
    )(tvec, *parts, *first)


def turn(v):
    r, c = v.shape
    if r % 128:
        v = jnp.concatenate([v, jnp.zeros(((-r) % 128, c), F32)], 0)
    if c % 128:
        v = jnp.concatenate([v, jnp.zeros((v.shape[0], (-c) % 128), F32)], 1)
    return v.T[:c, :r]


def copy_out(bufs, outs, sems):
    copies = [pltpu.make_async_copy(b, o, sems.at[i]) for i, (b, o) in enumerate(zip(bufs, outs))]
    for c in copies:
        c.start()
    for c in copies:
        c.wait()


def copied(shapes, *more):
    return dict(
        out_shape=tuple(jax.ShapeDtypeStruct(s, F32) for s in shapes),
        out_specs=(pl.BlockSpec(memory_space=pltpu.HBM),) * len(shapes),
        scratch_shapes=[pltpu.VMEM(s, F32) for s in shapes] + [pltpu.SemaphoreType.DMA((len(shapes),)), *more],
    )


def last_ffn_kernel(*refs):
    ins, results, (up_ref, down_ref, sems) = refs[:-5], refs[-5:-3], refs[-3:]
    for i, ref in enumerate((up_ref, down_ref)):
        total = ins[0][i].astype(F32)
        for r in ins[1:]:
            total += r[i].astype(F32)
        ref[...] = total
    copy_out((up_ref, down_ref), results, sems)


def last_ffn(parts):
    _, rows, f = parts[0].shape
    return pl.pallas_call(
        last_ffn_kernel,
        **copied([(rows, f), (rows, f)]),
        name="last_ffn",
    )(*parts)


def last_attn_kernel(nt, rows, cols, places, t_ref, *refs):
    ins, rest, sems, turn_ref = refs[: 2 * nt], refs[2 * nt : -2], refs[-2], refs[-1]
    results, outs = rest[: len(rest) // 2], rest[len(rest) // 2 :]
    turn_ref[...] = jnp.zeros_like(turn_ref)
    groups = []
    for g in range(2):
        total = ins[g * nt][...].astype(F32)
        for r in ins[g * nt + 1 : (g + 1) * nt]:
            total += r[...].astype(F32)
        groups.append(total)
    one, two = groups
    outs[0][...] = turn(one[:rows, :cols])
    outs[1][...] = one[:rows, cols:]
    outs[2][...] = two[:rows, :cols]
    outs[3][...] = two[:rows, cols:]
    pad = (one.shape[0] - rows) // 2
    small = []
    for i in range(2):
        at = rows + i * pad
        both = one[at : at + 2] + one[at + 2 : at + 4]
        small.append(jnp.where(t_ref[0] >= 2, both[1:2], both[0:1]))
    small = jnp.concatenate(small, 1)
    c = outs[4].shape[1]
    for ref, row in zip(outs[4:], places):
        n = ref.shape[0] if row < UB else ref.shape[1]
        for i in range(n):
            at = (row + i) * c
            turn_ref[i : i + 1, :c] = small[:, at : at + c]
        ref[...] = turn_ref[:n, :c] if row < UB else turn_ref[...].T[:c, :n]
    copy_out(outs, results, sems)


def last_attn(tvec, nt, rows, cols, places, shapes, one, two):
    out = [(cols, rows)] + [(rows, cols)] * 3 + list(shapes)
    spec = copied(out, pltpu.VMEM((128, 128), F32))
    return pl.pallas_call(
        partial(last_attn_kernel, nt, rows, cols, places),
        grid_spec=pltpu.PrefetchScalarGridSpec(
            num_scalar_prefetch=1,
            grid=(1,),
            in_specs=[pl.BlockSpec(p.shape, lambda i, t: (0, 0)) for p in (*one, *two)],
            out_specs=spec["out_specs"],
            scratch_shapes=spec["scratch_shapes"],
        ),
        out_shape=spec["out_shape"],
        name="last_attn",
    )(tvec, *one, *two)


def finish_kernel(dx_ref, r_ref, x_ref, mg_ref, vec_ref, lo_ref, o_ref, out_ref):
    grad = dx_ref[...] + r_ref[...].astype(F32)
    hat, inv = normalize(x_ref[...].astype(F32))
    done = (mg_ref[...] + norm_back(grad * replicated(vec_ref, FG), hat, inv)).astype(BF)
    p = by_parity(True)
    o_ref[...] = dot(p, done).astype(BF)
    out_ref[...] = dot(p, lo_ref[...]).astype(BF)


def finish(dx, received, x, middle_grad, vec, layer_output):
    rows = pl.BlockSpec((ROWS, D), lambda i: (0, 0))
    return pl.pallas_call(
        finish_kernel,
        grid=(1,),
        in_specs=[rows] * 4 + [pl.BlockSpec(vec.shape, lambda i: (0, 0)), rows],
        out_specs=(rows, rows),
        out_shape=(jax.ShapeDtypeStruct((ROWS, D), BF),) * 2,
        cost_estimate=pl.CostEstimate(
            flops=4 * ROWS * ROWS * D, bytes_accessed=16 * ROWS * D, transcendentals=0
        ),
        name="finish",
    )(dx, received, x, middle_grad, vec, layer_output)


def around_kernel(rows, cols, t_ref, *refs):
    ins, o_ref = refs[:-2], refs[-1]
    nt = len(ins)
    for t in range(nt):

        @pl.when(t_ref[0] == t)
        def _(t=t):
            block = [ins[(t - j) % nt] for j in range(nt)]
            for m in range(4):
                at = slice(m * cols, (m + 1) * cols)
                o_ref[:rows, m * D : (m + 1) * D] = jnp.concatenate([b[:rows, at] for b in block], 1)
            for j in range(nt):
                o_ref[rows:, j * 4 * cols : (j + 1) * 4 * cols] = block[j][rows:]


def assemble_around(tvec, rows, cols, blocks, first):
    nt, n = len(blocks), blocks[0].shape[0]
    return pl.pallas_call(
        partial(around_kernel, rows, cols),
        grid_spec=pltpu.PrefetchScalarGridSpec(
            num_scalar_prefetch=1,
            grid=(1,),
            in_specs=[pl.BlockSpec(b.shape, lambda i, t: (0, 0)) for b in blocks] + [HERE],
            out_specs=pl.BlockSpec((n, 4 * D), lambda i, t: (0, 0)),
        ),
        out_shape=jax.ShapeDtypeStruct((n, 4 * D), BF),
        name="around",
    )(tvec, *blocks, first)


def assemble_kernel(a_ref, qkv_ref, kv_ref, out_ref, small_ref):
    r = qkv_ref.shape[0]
    qkv_ref[...] = a_ref[:r, : 3 * D]
    kv_ref[...] = a_ref[:r, D : 3 * D]
    out_ref[...] = a_ref[:r, 3 * D :]
    small_ref[...] = a_ref[r:]


def assemble(n_dp, rows, a):
    _, full, n = a.shape

    def out(width):
        return pl.BlockSpec((rows, width), lambda j: (j, 0))

    return pl.pallas_call(
        assemble_kernel,
        grid=(n_dp,),
        in_specs=[pl.BlockSpec((None, full, n), lambda j: (j, 0, 0))],
        out_specs=(
            out(3 * D), out(2 * D), out(D),
            pl.BlockSpec((None, full - rows, n), lambda j: (j, 0, 0)),
        ),
        out_shape=(
            jax.ShapeDtypeStruct((D, 3 * D), BF),
            jax.ShapeDtypeStruct((D, 2 * D), BF),
            jax.ShapeDtypeStruct((D, D), BF),
            jax.ShapeDtypeStruct((n_dp, full - rows, n), BF),
        ),
        name="assemble",
    )(a)


def pack_kernel(x_ref, up_ref, down_ref, _, o_ref, ffn_ref):
    r = up_ref.shape[0]
    o_ref[:ROWS] = x_ref[...]
    for ref, at in ((o_ref, ROWS), (ffn_ref, 0)):
        ref[at : at + r] = up_ref[...]
        ref[at + r : at + 2 * r] = down_ref[...]


def pack(x, up, down_t, first):
    r, f = up.shape
    return pl.pallas_call(
        pack_kernel,
        in_specs=[pl.BlockSpec(memory_space=pltpu.VMEM)] * 3 + [HERE],
        out_shape=(jax.ShapeDtypeStruct((ROWS + 2 * r, f), BF), jax.ShapeDtypeStruct((2 * r, f), BF)),
        name="pack",
    )(x, up, down_t, first)


def order_kernel(t_ref, *refs):
    ins, o_ref = refs[:-2], refs[-1]
    nt = len(ins)
    for s in range(nt):
        o_ref[lax.rem(t_ref[0] - s + nt, nt)] = ins[s][...]


def order_ffn(tvec, rows, parts, first):
    f = parts[0].shape[1]

    def spec(p):
        return pl.BlockSpec((2 * rows, f), lambda i, t, j=p.shape[0] // (2 * rows) - 1: (j, 0))

    return pl.pallas_call(
        order_kernel,
        grid_spec=pltpu.PrefetchScalarGridSpec(
            num_scalar_prefetch=1,
            grid=(1,),
            in_specs=[spec(p) for p in parts] + [HERE],
            out_specs=pl.BlockSpec((len(parts), 2 * rows, f), lambda i, t: (0, 0, 0)),
        ),
        out_shape=jax.ShapeDtypeStruct((len(parts), 2 * rows, f), BF),
        name="order_ffn",
    )(tvec, *parts, first)


def in_order(t, nt, blocks):
    twice = jnp.stack(blocks[::-1] + blocks[:0:-1])
    return lax.dynamic_slice_in_dim(twice, nt - 1 - t, nt, 0)


def ring(nt, s):
    return [(i, (i + s) % nt) for i in range(nt)]


def swap(n, bits):
    return [(i, i ^ bits) for i in range(n)]


def body(
    n_dp,
    nt,
    layer_input,
    output_grad,
    query_weight,
    key_weight,
    value_weight,
    out_weight,
    up_weight,
    down_weight,
    query_bias,
    value_bias,
    inner_gain,
    out_bias,
    up_bias,
    hidden_gain,
    down_bias,
    first_gain,
    second_gain,
    head_offsets,
):
    t = lax.axis_index("tensor")
    tvec = t.reshape(1).astype(jnp.int32)
    right = [(i, i + 1) for i in range(nt - 1)]
    left = [(i + 1, i) for i in range(nt - 1)]

    rows, cols = query_weight.shape
    c = HD // n_dp
    split = [query_bias, value_bias, inner_gain, up_bias, hidden_gain]
    whole = [out_bias, down_bias, first_gain, second_gain]
    dp = lax.axis_index("dp").astype(jnp.int32)

    f = FF // nt
    layer_input = sort_rows(layer_input)
    output_grad = sort_rows(output_grad)

    places = [QB, VB, IG, UB, HG, OB, DB, FG, SG]
    vectors = split + whole
    pad = 16 + (-rows) % 16

    def padded(arrays, axis):
        out = []
        for a in arrays:
            gap = [(0, 0)] * a.ndim
            gap[axis] = (0, a.shape[axis] % 2)
            out.append(jnp.pad(a, gap) if a.shape[axis] % 2 else a)
        return out

    def packed(arrays, lead):
        shape = arrays[0].shape[:lead]
        head = jnp.concatenate(padded(arrays[:3], lead), lead)
        tail = jnp.concatenate([jnp.swapaxes(a, lead, lead + 1) for a in arrays[3:]], lead + 1)
        return jnp.concatenate([head.reshape(*shape, -1), tail.reshape(*shape, -1)], lead)

    small = jnp.concatenate([packed(vectors, 0), head_offsets.astype(BF).reshape(-1)])
    small = jnp.pad(small, (0, 4 * cols - small.shape[0])).reshape(1, 4 * cols)
    small = jnp.pad(small, ((0, pad - 1), (0, 0)))
    mine = jnp.concatenate([query_weight, key_weight, value_weight, out_weight.T], 1)
    mine = jnp.concatenate([mine, small], 0)
    around = [mine] + [lax.ppermute(mine, "tensor", ring(nt, s)) for s in range(1, nt)]
    if rows % 16:
        around = in_order(t, nt, around)
        small_z = around[:, rows:].transpose(1, 0, 2).reshape(pad, 4 * D)
        around = around[:, :rows].reshape(nt, rows, 4, cols).transpose(1, 2, 0, 3)
        around = jnp.concatenate([around.reshape(rows, 4 * D), small_z], 0)
    else:
        around = assemble_around(tvec, rows, cols, around, layer_input)
    mine = lax.all_gather(around, "dp", axis=0)

    if rows % 16:
        ffn = jnp.concatenate([up_weight, down_weight.T], 0)
        both = jnp.concatenate([layer_input, ffn], 0)
    else:
        both, ffn = pack(layer_input, up_weight, down_weight.T, around)
    one = lax.ppermute(both, "tensor", ring(nt, 1))
    ffn = [both, one] + [lax.ppermute(ffn, "tensor", ring(nt, s)) for s in range(2, nt)]
    x = [layer_input, one]
    for s in range(2, nt):
        x.append(lax.ppermute(x[-1][:ROWS], "tensor", right[s - 1 :]))
    if rows % 16:
        w4, small = mine[:, :rows].reshape(D, 4 * D), mine[:, rows:]
        w_qkv, w_kv, w_out_t = w4[:, : 3 * D], w4[:, D : 3 * D], w4[:, 3 * D :]
        ffn = in_order(t, nt, [a[-2 * rows :] for a in ffn])
        ffn = lax.all_gather(ffn, "dp", axis=0).reshape(n_dp, nt, 2, rows, f)
        ffn = ffn.transpose(1, 2, 0, 3, 4).reshape(1, nt, 2, D, f)
    else:
        w_qkv, w_kv, w_out_t, small = assemble(n_dp, rows, mine)
        ffn = order_ffn(tvec, rows, ffn, w_kv)
        ffn = lax.all_gather(ffn, "dp", axis=0).reshape(n_dp, nt, 2, rows, f)
    small = small[:, 0].reshape(n_dp, nt, 4 * cols)
    at = VECTOR_ROWS * c
    head = small[:, :, : UB * c].reshape(n_dp, nt, UB, c).transpose(1, 2, 0, 3)
    tail = small[:, :, UB * c : at].reshape(n_dp, nt, c, VECTOR_ROWS - UB).transpose(1, 3, 0, 2)
    vec = jnp.concatenate([head.reshape(nt, -1), tail.reshape(nt, -1)], 1).astype(F32)
    offsets = small[0, :, at : at + head_offsets.size].astype(jnp.int32).reshape(HEADS, -1)

    n0, own = project(x[0], vec, w_qkv)
    normed, others = [n0], []
    for s in range(1, nt):
        ns, kv = project(x[s], vec, w_kv)
        normed.append(ns)
        others.append(kv)
    aq = query_columns(t, offsets)
    ak = jnp.stack([key_columns(t - s) for s in range(nt)])
    context, qq = attend(tvec, own, others, aq, ak)

    g = output_grad
    layer_output, n2, hn, pg, inner_normed, branch_grad, middle_grad, wide, sum_d, sum_f = middle_layer(
        nt, context, layer_input, g, w_out_t, ffn, vec
    )
    d_second_gain, d_out_bias, d_down_bias, d_inner_gain = (sum_d[i] for i in range(4))
    d_up_bias, d_hidden_gain = sum_f[0], sum_f[1]

    core = (dp % 2).reshape(1)
    nb = n_dp if rows % 16 == 0 else 1
    outs = 2 if n_dp == 8 else 1
    other = swap(n_dp, 1)
    dks, dvs, sums = [None] * nt, [None] * nt, [None] * nt
    dq, received, have_ffn, dx = None, None, None, None
    if n_dp == 8:
        order = (dp // 2) ^ jnp.arange(4, dtype=jnp.int32)
    def over_tensor(parts):
        return [parts[0]] + [lax.ppermute(parts[s], "tensor", ring(nt, s)) for s in range(1, nt)]

    def over_chips(parts):
        return [parts[0]] + [lax.ppermute(parts[o], "dp", swap(8, 2 * o)) for o in (1, 2, 3)]

    d_ffn = ffn_outer(core, nt, nb, outs, n2, pg, g, hn)
    if n_dp == 8:
        have_ffn = halve(order, d_ffn[0], lax.ppermute(d_ffn[1], "dp", other))
        got_ffn = over_chips(have_ffn)
    for s in reversed(range(nt)):
        kv = own if s == 0 else others[s - 1]
        w = w_qkv if s == 0 else w_kv
        first = [d_ffn[0]] if s == nt - 1 else [sent]
        if s == nt - 2 and have_ffn is not None:
            first = [have_ffn[0]]
        dq, dks[s], dvs[s], dx, sums[s] = attend_back(tvec, s, qq, wide, kv, ak, dq, w, x[s], first)
        if s > 0:
            if received is not None:
                dx = (dx.astype(F32) + received.astype(F32)).astype(BF)
            received = lax.ppermute(dx, "tensor", left[s - 1 :])
            sent = dx
    input_grad, layer_output = finish(dx, received, x[0], middle_grad, vec, layer_output)
    sums = sum(sums[1:], sums[0])

    d_small = [sums[0], sums[1], d_inner_gain, d_up_bias, d_hidden_gain]
    d_whole = [d_out_bias, d_down_bias, sums[2], d_second_gain]
    cut = [a.reshape(nt, -1, n_dp, c) for a in d_small]
    same = [jnp.broadcast_to(a.reshape(1, -1, n_dp, c), (nt, a.size // HD, n_dp, c)) for a in d_whole]
    d_small = jnp.concatenate(padded(cut + same, 1), 1).transpose(2, 0, 1, 3).reshape(n_dp, 1, nt, -1)
    d_small = jnp.pad(d_small, ((0, 0), (0, 0), (0, 0), (0, 4 * cols - d_small.shape[-1])))
    high = lax.reduce_precision(d_small, 8, 7)
    d_small = jnp.concatenate([high, d_small - high], 1).astype(BF)
    first = [received]
    if n_dp == 8:
        sum_ffn = chips(tvec, nt, got_ffn, first=[dq])
        first.append(sum_ffn[0])
        d_small = d_small.reshape(4, 2, 4, 2 * D)
        d_small = jnp.pad(d_small, ((0, 0), (0, 0), (0, pad - 4), (0, 0)))
        give = lax.dynamic_index_in_dim(d_small, 1 - core[0], 1, False)
        keep = lax.dynamic_index_in_dim(d_small, core[0], 1, False)
        first += [give, keep]
    d_one = attn_outer(core, nb, outs, [[(branch_grad, inner_normed)], [(n0, dq)]], first)
    d_two = attn_outer(core, nb, outs, [list(zip(normed, dks)), list(zip(normed, dvs))], d_one[:1])

    if n_dp == 8:

        d_ffn = last_ffn(over_tensor(sum_ffn))
        small = (keep, lax.ppermute(give, "dp", other))
        d_one = halve(order, d_one[0], lax.ppermute(d_one[1], "dp", other), small)
        d_two = halve(order, d_two[0], lax.ppermute(d_two[1], "dp", other), ())
        d_one = over_tensor(chips(tvec, nt, over_chips(d_one), (rows, cols)))
        d_two = over_tensor(chips(tvec, nt, over_chips(d_two), (rows, cols)))
        shapes = [a.shape if i < 3 else a.shape[::-1] for i, a in enumerate(vectors)]
        g_o, g_q, g_k, g_v, *pieces = last_attn(tvec, nt, rows, cols, places, shapes, d_one, d_two)
        pieces = pieces[:3] + [a.T for a in pieces[3:]]
        d_up, d_down = d_ffn[0], d_ffn[1].T
    else:
        d_ffn = d_ffn[0]
        if nb == 1:
            d_ffn = d_ffn.reshape(nt, 2, n_dp, rows, f).transpose(2, 0, 1, 3, 4)
        d_ffn = lax.psum_scatter(d_ffn, "dp", scatter_dimension=0)
        d_ffn = lax.psum_scatter(d_ffn, "tensor", scatter_dimension=0).astype(F32)
        d_small = jnp.pad(d_small.reshape(n_dp, 2, 4 * D), ((0, 0), (0, pad - 2), (0, 0)))
        d4 = jnp.concatenate([d_one[0], d_two[0]], -1).reshape(n_dp, rows, 4 * D)
        d4 = jnp.concatenate([d4, d_small], 1)
        d4 = lax.psum_scatter(d4, "dp", scatter_dimension=0)
        small_z = d4[rows:].reshape(pad, nt, 4 * cols).transpose(1, 0, 2)
        d4 = d4[:rows].reshape(rows, 4, nt, cols).transpose(2, 0, 1, 3).reshape(nt, rows, 4 * cols)
        d4 = jnp.concatenate([d4, small_z], 1)
        total = lax.psum_scatter(d4, "tensor", scatter_dimension=0).astype(F32)
        g_o, g_q, g_k, g_v = (total[:rows, i * cols : (i + 1) * cols] for i in range(4))
        g_o, d_up, d_down = g_o.T, d_ffn[0], d_ffn[1].T
        out = total[rows] + total[rows + 1]
        pieces = [
            out[row * c : (row + a.shape[0]) * c].reshape(a.shape) for a, row in zip(vectors, places)
        ]
    p_qb, p_vb, p_ig, p_ub, p_hg, p_ob, p_db, p_fg, p_sg = pieces
    return (
        layer_output,
        input_grad,
        g_q,
        g_k,
        g_v,
        g_o,
        d_up,
        d_down,
        p_qb,
        p_vb,
        p_ig,
        p_ob,
        p_ub,
        p_hg,
        p_db,
        p_fg,
        p_sg,
    )


def solution(mesh):
    tokens = P(("dp", "tensor"), None)
    dt = P("dp", "tensor")
    td = P("tensor", "dp")
    nd = P(None, "dp")
    in_specs = (tokens, tokens, dt, dt, dt, td, dt, td, td, td, td, nd, td, td, nd, nd, nd, P("tensor", None))
    out_specs = (tokens, tokens, dt, dt, dt, td, dt, td, td, td, td, nd, td, td, nd, nd, nd)
    return jax.shard_map(
        partial(body, mesh.shape["dp"], mesh.shape["tensor"]),
        mesh=mesh,
        in_specs=in_specs,
        out_specs=out_specs,
        check_vma=False,
    )
```

profile of v0, /device:TPU:0, one launch (start us, length us, event | category | flops | bytes accessed | tf_op | source)
XLA Modules:
  0.0 458.4 jit_solution(6981228405867778720)
XLA Ops:
  22.1 6.5 %collective-permute-done.1.refs_2_ = bf16[112,768]{1,0:T(8,128)(2,1)S(1)} collective-permute-done((bf16[112,768]{1,0:T(8,128)(2,1)S(1)}, bf16[112,768]{1,0:T(8,128)(2,1)S(1)}, u32[]{:S(2)}, u32[]{:S(2)}) %collective-permute-start.1) | collective-permute-done | bytes 172064 | tf_op jit(solution)/shard_map/ppermute | solution.py:1148
  34.3 4.1 collective-permute-start.3
  40.8 36.0 %all-gather.5.cloned.1.call-done = bf16[896,3072]{1,0:T(8,128)(2,1)} async-done(((bf16[112,3072]{1,0:T(8,128)(2,1)}), bf16[896,3072]{1,0:T(8,128)(2,1)}) %all-gather.5.cloned.1.call-update) | async-done | bytes 5505040 | tf_op jit(solution)/shard_map/all_gather | solution.py:1156
  76.8 7.7 %assemble.1 = (bf16[768,2304]{1,0:T(8,128)(2,1)}, bf16[768,1536]{1,0:T(8,128)(2,1)}, bf16[768,768]{1,0:T(8,128)(2,1)}, bf16[8,16,3072]{2,1,0:T(8,128)(2,1)}) custom-call(bf16[8,112,3072]{2,1,0:T(8,128)(2,1)} %bitcast.35), custom_call_target="tpu_custom_call" | custom-call | tf_op jit(solution)/shard_map/assemble/pallas_call | solution.py:1013
  110.3 5.9 %project.5 = (bf16[768,768]{1,0:T(8,128)(2,1)}, bf16[768,1536]{1,0:T(8,128)(2,1)}) custom-call(bf16[960,768]{1,0:T(8,128)(2,1)} %copy-done, f32[4,5376]{1,0:T(4,128)} %maximum_convert_fusion.vec_ref, bf16[768,1536]{1,0:T(8,128)(2,1)} %get-tuple-element.114.w_ref.refs_4_.r_6_.r_7_), custom_call_target="tpu_custom_call" | custom-call | flops 1811939328 | bytes 7077888 | tf_op jit(solution)/shard_map/project/pallas_call | solution.py:109
  116.2 5.9 %project.6 = (bf16[768,768]{1,0:T(8,128)(2,1)}, bf16[768,1536]{1,0:T(8,128)(2,1)}) custom-call(bf16[768,768]{1,0:T(8,128)(2,1)} %collective-permute-done.4.x_ref.r_8_, f32[4,5376]{1,0:T(4,128)} %maximum_convert_fusion.vec_ref, bf16[768,1536]{1,0:T(8,128)(2,1)} %get-tuple-element.114.w_ref.refs_4_.r_6_.r_7_), custom_call_target="tpu_custom_call" | custom-call | flops 1811939328 | bytes 7077888 | tf_op jit(solution)/shard_map/project/pallas_call | solution.py:109
  122.1 6.4 %project.7 = (bf16[768,768]{1,0:T(8,128)(2,1)}, bf16[768,1536]{1,0:T(8,128)(2,1)}) custom-call(bf16[768,768]{1,0:T(8,128)(2,1)} %collective-permute-done.5.x_ref.r_7_, f32[4,5376]{1,0:T(4,128)} %maximum_convert_fusion.vec_ref, bf16[768,1536]{1,0:T(8,128)(2,1)} %get-tuple-element.114.w_ref.refs_4_.r_6_.r_7_), custom_call_target="tpu_custom_call" | custom-call | flops 1811939328 | bytes 7077888 | tf_op jit(solution)/shard_map/project/pallas_call | solution.py:109
  128.5 7.0 %project.4 = (bf16[768,768]{1,0:T(8,128)(2,1)}, bf16[768,2304]{1,0:T(8,128)(2,1)}) custom-call(bf16[768,768]{1,0:T(8,128)(2,1)} %sort_rows.2.refs_4_.x_ref.r_8_, f32[4,5376]{1,0:T(4,128)} %maximum_convert_fusion.vec_ref, bf16[768,2304]{1,0:T(8,128)(2,1)} %get-tuple-element.111.w_ref.r_7_), custom_call_target="tpu_custom_call" | custom-call | flops 2717908992 | bytes 9437184 | tf_op jit(solution)/shard_map/project/pallas_call | solution.py:109
  135.5 17.5 %attend.1 = (f32[768,768]{1,0:T(8,128)}, bf16[768,1536]{1,0:T(8,128)(2,1)}) custom-call(s32[1]{0:T(128)} %bitcast.t_ref.r_0_, bf16[768,2304]{1,0:T(8,128)(2,1)} %get-tuple-element.112.q_ref.refs_0_.refs_4_.r_3_.r_4_, bf16[768,768]{1,0:T(8,128)(2,1)} %copy.49.aq_ref, bf16[768,2304]{1,0:T(8,128)(2,1)} %get-tuple-element.112.q_ref.refs_0_.refs_4_.r_3_.r_4_, ...), custom_call_target="tpu_custom_call" | custom-call | flops 16000000000 | bytes 16777216 | tf_op jit(solution)/shard_map/attend/pallas_call | solution.py:325
  153.0 41.0 %middle.1 = (bf16[768,768]{1,0:T(8,128)(2,1)}, bf16[768,768]{1,0:T(8,128)(2,1)}, bf16[768,3072]{1,0:T(8,128)(2,1)}, bf16[768,3072]{1,0:T(8,128)(2,1)}, bf16[768,...) custom-call(f32[768,768]{1,0:T(8,128)} %get-tuple-element.119.c_ref,, ...), custom_call_target="tpu_custom_call" | custom-call | flops 16307453952 | bytes 31457280 | tf_op jit(solution)/shard_map/middle/pallas_call | solution.py:635
  194.0 15.5 %ffn_outer.1 = (bf16[4,4,2,96,768]{4,3,2,1,0:T(8,128)(2,1)}, bf16[4,4,2,96,768]{4,3,2,1,0:T(8,128)(2,1)}) custom-call(s32[1]{0:T(128)} %bitcast.14.core_ref, bf16[768,768]{1,0:T(8,128)(2,1)} %get-tuple-element.123.n2_ref, bf16[768,3072]{1,0:T(8,128)(2,1)} %get-tuple-element.124.pg_ref, bf16[768,768]{1,0:T(8,128)(2,1)} %sort_rows.3.g_ref, ...), custom_call_target="tpu_custom_call" | custom-call | flops 7247757312 | bytes 18874368 | tf_op jit(solution)/shard_map/ffn_outer/pallas_call | solution.py:689
  210.1 6.4 %attend_back.4 = (f32[768,768]{1,0:T(8,128)}, bf16[768,768]{1,0:T(8,128)(2,1)}, bf16[768,768]{1,0:T(8,128)(2,1)}, bf16[768,768]{1,0:T(8,128)(2,1)}, f32[8,768]{1,0:T(8,128)}) custom-call(s32[1]{0:T(128)} %bitcast.t_ref.r_0_, bf16[768,1536]{1,0:T(8,128)(2,1)} %get-tuple-element.118.r_1_, bf16[768,1536]{1,0:T(8,128)(2,1)} %get-tuple-element.122.r_2_, ...), custom_call_target="tpu_custom_call" | custom-call | flops 16000000000 | bytes 16777216 | tf_op jit(solution)/shard_map/attend_back/pallas_call | solution.py:469
  223.9 7.2 %halve.3 = (bf16[4,2,96,768]{3,2,1,0:T(8,128)(2,1)}, bf16[4,2,96,768]{3,2,1,0:T(8,128)(2,1)}, bf16[4,2,96,768]{3,2,1,0:T(8,128)(2,1)}, bf16[4,2,96,768]{3,2,1,0:T(8,128)(2,1)}) custom-call(s32[4]{0:T(128)} %iota_xor_fusion.order_ref, bf16[4,4,2,96,768]{4,3,2,1,0:T(8,128)(2,1)} %get-tuple-element.126.r_8_.refs_0_, ...), custom_call_target="tpu_custom_call" | custom-call | flops 2359296 | bytes 14155776 | tf_op jit(solution)/shard_map/halve/pallas_call | solution.py:783
  231.1 7.8 %attend_back.5 = (f32[768,768]{1,0:T(8,128)}, bf16[768,768]{1,0:T(8,128)(2,1)}, bf16[768,768]{1,0:T(8,128)(2,1)}, bf16[768,768]{1,0:T(8,128)(2,1)}, f32[8,768]{1,0:T(8,128)}) custom-call(s32[1]{0:T(128)} %bitcast.t_ref.r_0_, bf16[768,1536]{1,0:T(8,128)(2,1)} %get-tuple-element.118.r_1_, bf16[768,1536]{1,0:T(8,128)(2,1)} %get-tuple-element.122.r_2_, ...), custom_call_target="tpu_custom_call" | custom-call | flops 16000000000 | bytes 16777216 | tf_op jit(solution)/shard_map/attend_back/pallas_call | solution.py:469
  244.8 8.1 %attend_back.6 = (f32[768,768]{1,0:T(8,128)}, bf16[768,768]{1,0:T(8,128)(2,1)}, bf16[768,768]{1,0:T(8,128)(2,1)}, bf16[768,768]{1,0:T(8,128)(2,1)}, f32[8,768]{1,0:T(8,128)}) custom-call(s32[1]{0:T(128)} %bitcast.t_ref.r_0_, bf16[768,1536]{1,0:T(8,128)(2,1)} %get-tuple-element.118.r_1_, bf16[768,1536]{1,0:T(8,128)(2,1)} %get-tuple-element.122.r_2_, ...), custom_call_target="tpu_custom_call" | custom-call | flops 16000000000 | bytes 16777216 | tf_op jit(solution)/shard_map/attend_back/pallas_call | solution.py:469
  255.9 24.2 %attend_back.7 = (bf16[768,768]{1,0:T(8,128)(2,1)}, bf16[768,768]{1,0:T(8,128)(2,1)}, bf16[768,768]{1,0:T(8,128)(2,1)}, f32[768,768]{1,0:T(8,128)}, f32[8,768]{1,0:T(8,128)}) custom-call(s32[1]{0:T(128)} %bitcast.t_ref.r_0_, bf16[768,1536]{1,0:T(8,128)(2,1)} %get-tuple-element.118.r_1_, bf16[768,1536]{1,0:T(8,128)(2,1)} %get-tuple-element.122.r_2_, ...), custom_call_target="tpu_custom_call" | custom-call | flops 16000000000 | bytes 16777216 | tf_op jit(solution)/shard_map/attend_back/pallas_call | solution.py:469
  283.6 12.5 %collective-permute-done.13.refs_2_ = bf16[4,2,96,768]{3,2,1,0:T(8,128)(2,1)} collective-permute-done((bf16[4,2,96,768]{3,2,1,0:T(8,128)(2,1)}, bf16[4,2,96,768]{3,2,1,0:T(8,128)(2,1)}, u32[]{:S(2)}, u32[]{:S(2)}) %collective-permute-start.13) | collective-permute-done | bytes 1179680 | tf_op jit(solution)/shard_map/ppermute | solution.py:1214
  300.7 65.3 %collective-permute-done.11.r_ref.refs_4_ = bf16[768,768]{1,0:T(8,128)(2,1)} collective-permute-done((bf16[768,768]{1,0:T(8,128)(2,1)S(1)}, bf16[768,768]{1,0:T(8,128)(2,1)}, u32[]{:S(2)}, u32[]{:S(2)}) %collective-permute-start.11) | collective-permute-done | bytes 1179680 | tf_op jit(solution)/shard_map/ppermute | solution.py:1230
  366.0 6.0 %attn_outer.2 = (bf16[4,96,1536]{2,1,0:T(8,128)(2,1)}, bf16[4,96,1536]{2,1,0:T(8,128)(2,1)}) custom-call(s32[1]{0:T(128)} %bitcast.14.core_ref, bf16[768,768]{1,0:T(8,128)(2,1)} %get-tuple-element.140.refs_0_, bf16[768,768]{1,0:T(8,128)(2,1)} %get-tuple-element.141.refs_1_, bf16[768,768]{1,0:T(8,128)(2,1)} %get-tuple-element.142.refs_2_.refs_0_, ...), custom_call_target="tpu_custom_call" | custom-call | flops 1811939328 | bytes 4718592 | tf_op jit(solution)/shard_map/attn_outer/pallas_call | solution.py:736
  372.0 14.2 %attn_outer.3 = (bf16[4,96,1536]{2,1,0:T(8,128)(2,1)}, bf16[4,96,1536]{2,1,0:T(8,128)(2,1)}) custom-call(s32[1]{0:T(128)} %bitcast.14.core_ref, bf16[768,768]{1,0:T(8,128)(2,1)} %get-tuple-element.142.refs_2_.refs_0_, bf16[768,768]{1,0:T(8,128)(2,1)} %get-tuple-element.164.refs_1_, bf16[768,768]{1,0:T(8,128)(2,1)} %get-tuple-element.165.refs_2_, ...), custom_call_target="tpu_custom_call" | custom-call | flops 7247757312 | bytes 14155776 | tf_op jit(solution)/shard_map/attn_outer/pallas_call | solution.py:736
  386.8 6.3 %collective-permute-start.30 = (bf16[2,96,768]{2,1,0:T(8,128)(2,1)}, bf16[2,96,768]{2,1,0:T(8,128)(2,1)S(1)}, u32[]{:S(2)}, u32[]{:S(2)}) collective-permute-start(bf16[2,96,768]{2,1,0:T(8,128)(2,1)} %get-tuple-element.189), channel_id=1, source_target_pairs={{0,1},{1,2},{2,3},{3,0},{4,5},{5,6},{6,7},{7,4},{8,9},{9,10},{10,1... | collective-permute-start | bytes 884744 | tf_op jit(solution)/shard_map/ppermute | solution.py:1211
  401.3 4.1 collective-permute-start.31
  415.7 3.9 collective-permute-start.32
  440.6 7.7 %finish.1 = (bf16[768,768]{1,0:T(8,128)(2,1)}, bf16[768,768]{1,0:T(8,128)(2,1)}) custom-call(f32[768,768]{1,0:T(8,128)} %get-tuple-element.135.dx_ref, bf16[768,768]{1,0:T(8,128)(2,1)} %collective-permute-done.11.r_ref.refs_4_, bf16[768,768]{1,0:T(8,128)(2,1)} %sort_rows.2.refs_4_.x_ref.r_8_, f32[768,768]{1,0:T(8,128)} %get-tuple-element.136.mg_ref, ...), custom_call_target="tpu_custom_call" | custom-call | flops 1811939328 | bytes 9437184 | tf_op jit(solution)/shard_map/finish/pallas_call | solution.py:956
  (268 shorter events, 115.9 us)
Async XLA Ops:
  7.2 69.6 %all-gather.5.cloned.1.call-start = ((), (), s32[]{:S(2)}) async-start(), calls=%async_computation | async-start | bytes 6193152 | tf_op jit(solution)/shard_map/all_gather | solution.py:1156
  31.6 121.4 %all-gather.7.cloned.1.call-start = ((), (), s32[]{:S(2)}) async-start(), calls=%async_computation.1 | async-start | bytes 10616832 | tf_op jit(solution)/shard_map/all_gather | solution.py:1177
  34.3 50.3 %collective-permute-start.3 = (bf16[960,768]{1,0:T(8,128)(2,1)}, bf16[960,768]{1,0:T(8,128)(2,1)S(1)}, u32[]{:S(2)}, u32[]{:S(2)}) collective-permute-start(bf16[960,768]{1,0:T(8,128)(2,1)} %get-tuple-element.113.refs_0_), channel_id=1, source_target_pairs={{0,1},{1,2},{2,3},{3,0},{4,5},{5,6},{6,7},{7,4},{8,9},{9,10},{10,1... | collective-permute-start | bytes 4423688 | tf_op jit(solution)/shard_map/ppermute | solution.py:1163
  38.4 46.1 %collective-permute-start.6 = (bf16[192,768]{1,0:T(8,128)(2,1)}, bf16[192,768]{1,0:T(8,128)(2,1)S(1)}, u32[]{:S(2)}, u32[]{:S(2)}) collective-permute-start(bf16[192,768]{1,0:T(8,128)(2,1)} %get-tuple-element.121), channel_id=1, source_target_pairs={{0,2},{1,3},{2,0},{3,1},{4,6},{5,7},{6,4},{7,5},{8,10},{9,11},{10,... | collective-permute-start | bytes 884744 | tf_op jit(solution)/shard_map/ppermute | solution.py:1164
  40.1 44.5 %collective-permute-start.7 = (bf16[192,768]{1,0:T(8,128)(2,1)}, bf16[192,768]{1,0:T(8,128)(2,1)S(1)}, u32[]{:S(2)}, u32[]{:S(2)}) collective-permute-start(bf16[192,768]{1,0:T(8,128)(2,1)} %get-tuple-element.121), channel_id=1, source_target_pairs={{0,3},{1,0},{2,1},{3,2},{4,7},{5,4},{6,5},{7,6},{8,11},{9,8},{10,9... | collective-permute-start | bytes 884744 | tf_op jit(solution)/shard_map/ppermute | solution.py:1164
  99.0 23.1 %collective-permute-start.5 = (bf16[768,768]{1,0:T(8,128)(2,1)}, bf16[768,768]{1,0:T(8,128)(2,1)}, u32[]{:S(2)}, u32[]{:S(2)}) collective-permute-start(bf16[768,768]{1,0:T(8,128)(2,1)} %collective-permute-done.4.x_ref.r_8_), channel_id=1, source_target_pairs={{2,3},{6,7},{10,11},{14,15},{18,19},{22,23},{26,27},{30,31}} | collective-permute-start | bytes 3538952 | tf_op jit(solution)/shard_map/ppermute | solution.py:1167
  209.4 14.5 %collective-permute-start.8 = (bf16[4,4,2,96,768]{4,3,2,1,0:T(8,128)(2,1)}, bf16[4,4,2,96,768]{4,3,2,1,0:T(8,128)(2,1)}, u32[]{:S(2)}, u32[]{:S(2)}) collective-permute-start(bf16[4,4,2,96,768]{4,3,2,1,0:T(8,128)(2,1)} %get-tuple-element.128), channel_id=1, source_target_pairs={{0,4},{4,0},{8,12},{12,8},{16,20},{20,16},{24,28},{28,24},{1,5},{5... | collective-permute-start | bytes 14155784 | tf_op jit(solution)/shard_map/ppermute | solution.py:1218
  216.5 22.5 %collective-permute-start.9 = (bf16[768,768]{1,0:T(8,128)(2,1)}, bf16[768,768]{1,0:T(8,128)(2,1)S(1)}, u32[]{:S(2)}, u32[]{:S(2)}) collective-permute-start(bf16[768,768]{1,0:T(8,128)(2,1)} %get-tuple-element.132), channel_id=1, source_target_pairs={{3,2},{7,6},{11,10},{15,14},{19,18},{23,22},{27,26},{31,30}} | collective-permute-start | bytes 3538952 | tf_op jit(solution)/shard_map/ppermute | solution.py:1230
  241.3 42.3 %collective-permute-start.12 = (bf16[4,2,96,768]{3,2,1,0:T(8,128)(2,1)}, bf16[4,2,96,768]{3,2,1,0:T(8,128)(2,1)}, u32[]{:S(2)}, u32[]{:S(2)}) collective-permute-start(bf16[4,2,96,768]{3,2,1,0:T(8,128)(2,1)} %get-tuple-element.144), channel_id=1, source_target_pairs={{0,8},{4,12},{8,0},{12,4},{16,24},{20,28},{24,16},{28,20},{1,9},{5... | collective-permute-start | bytes 3538952 | tf_op jit(solution)/shard_map/ppermute | solution.py:1214
  242.6 53.4 %collective-permute-start.13 = (bf16[4,2,96,768]{3,2,1,0:T(8,128)(2,1)}, bf16[4,2,96,768]{3,2,1,0:T(8,128)(2,1)}, u32[]{:S(2)}, u32[]{:S(2)}) collective-permute-start(bf16[4,2,96,768]{3,2,1,0:T(8,128)(2,1)} %get-tuple-element.145), channel_id=1, source_target_pairs={{0,16},{4,20},{8,24},{12,28},{16,0},{20,4},{24,8},{28,12},{1,17},{... | collective-permute-start | bytes 3538952 | tf_op jit(solution)/shard_map/ppermute | solution.py:1214
  243.2 52.9 %collective-permute-start.14 = (bf16[4,2,96,768]{3,2,1,0:T(8,128)(2,1)}, bf16[4,2,96,768]{3,2,1,0:T(8,128)(2,1)}, u32[]{:S(2)}, u32[]{:S(2)}) collective-permute-start(bf16[4,2,96,768]{3,2,1,0:T(8,128)(2,1)} %get-tuple-element.146), channel_id=1, source_target_pairs={{0,24},{4,28},{8,16},{12,20},{16,8},{20,12},{24,0},{28,4},{1,25},{... | collective-permute-start | bytes 3538952 | tf_op jit(solution)/shard_map/ppermute | solution.py:1214
  254.5 111.5 %collective-permute-start.11 = (bf16[768,768]{1,0:T(8,128)(2,1)S(1)}, bf16[768,768]{1,0:T(8,128)(2,1)}, u32[]{:S(2)}, u32[]{:S(2)}) collective-permute-start(bf16[768,768]{1,0:T(8,128)(2,1)S(1)} %add_convert_fusion.r_9_), channel_id=1, source_target_pairs={{1,0},{2,1},{3,2},{5,4},{6,5},{7,6},{9,8},{10,9},{11,10},{13,12},{... | collective-permute-start | bytes 3538952 | tf_op jit(solution)/shard_map/ppermute | solution.py:1230
  386.2 14.9 %collective-permute-start.15 = (bf16[4,96,1536]{2,1,0:T(8,128)(2,1)}, bf16[4,96,1536]{2,1,0:T(8,128)(2,1)S(1)}, u32[]{:S(2)}, u32[]{:S(2)}) collective-permute-start(bf16[4,96,1536]{2,1,0:T(8,128)(2,1)} %get-tuple-element.155), channel_id=1, source_target_pairs={{0,4},{4,0},{8,12},{12,8},{16,20},{20,16},{24,28},{28,24},{1,5},{5... | collective-permute-start | bytes 3538952 | tf_op jit(solution)/shard_map/ppermute | solution.py:1259
  386.8 13.9 %collective-permute-start.16 = (bf16[4,16,1536]{2,1,0:T(8,128)(2,1)}, bf16[4,16,1536]{2,1,0:T(8,128)(2,1)S(1)}, u32[]{:S(2)}, u32[]{:S(2)}) collective-permute-start(bf16[4,16,1536]{2,1,0:T(8,128)(2,1)} %get-tuple-element.221.refs_6_), channel_id=1, source_target_pairs={{0,4},{4,0},{8,12},{12,8},{16,20},{20,16},{24,28},{28,24},{1,5},{5... | collective-permute-start | bytes 589832 | tf_op jit(solution)/shard_map/ppermute | solution.py:1258
  386.8 21.9 %collective-permute-start.30 = (bf16[2,96,768]{2,1,0:T(8,128)(2,1)}, bf16[2,96,768]{2,1,0:T(8,128)(2,1)S(1)}, u32[]{:S(2)}, u32[]{:S(2)}) collective-permute-start(bf16[2,96,768]{2,1,0:T(8,128)(2,1)} %get-tuple-element.189), channel_id=1, source_target_pairs={{0,1},{1,2},{2,3},{3,0},{4,5},{5,6},{6,7},{7,4},{8,9},{9,10},{10,1... | collective-permute-start | bytes 884744 | tf_op jit(solution)/shard_map/ppermute | solution.py:1211
  399.1 15.6 %collective-permute-start.25 = (bf16[96,1536]{1,0:T(8,128)(2,1)}, bf16[96,1536]{1,0:T(8,128)(2,1)S(1)}, u32[]{:S(2)}, u32[]{:S(2)}) collective-permute-start(bf16[96,1536]{1,0:T(8,128)(2,1)} %get-tuple-element.179), channel_id=1, source_target_pairs={{0,16},{4,20},{8,24},{12,28},{16,0},{20,4},{24,8},{28,12},{1,17},{... | collective-permute-start | bytes 884744 | tf_op jit(solution)/shard_map/ppermute | solution.py:1214
  400.6 15.1 %collective-permute-start.26 = (bf16[96,1536]{1,0:T(8,128)(2,1)}, bf16[96,1536]{1,0:T(8,128)(2,1)}, u32[]{:S(2)}, u32[]{:S(2)}) collective-permute-start(bf16[96,1536]{1,0:T(8,128)(2,1)} %get-tuple-element.180), channel_id=1, source_target_pairs={{0,24},{4,28},{8,16},{12,20},{16,8},{20,12},{24,0},{28,4},{1,25},{... | collective-permute-start | bytes 884744 | tf_op jit(solution)/shard_map/ppermute | solution.py:1214
  401.3 20.5 %collective-permute-start.31 = (bf16[2,96,768]{2,1,0:T(8,128)(2,1)}, bf16[2,96,768]{2,1,0:T(8,128)(2,1)S(1)}, u32[]{:S(2)}, u32[]{:S(2)}) collective-permute-start(bf16[2,96,768]{2,1,0:T(8,128)(2,1)} %get-tuple-element.190), channel_id=1, source_target_pairs={{0,2},{1,3},{2,0},{3,1},{4,6},{5,7},{6,4},{7,5},{8,10},{9,11},{10,... | collective-permute-start | bytes 884744 | tf_op jit(solution)/shard_map/ppermute | solution.py:1211
  408.8 21.8 %collective-permute-start.17 = (bf16[112,1536]{1,0:T(8,128)(2,1)}, bf16[112,1536]{1,0:T(8,128)(2,1)S(1)}, u32[]{:S(2)}, u32[]{:S(2)}) collective-permute-start(bf16[112,1536]{1,0:T(8,128)(2,1)} %get-tuple-element.157), channel_id=1, source_target_pairs={{0,8},{4,12},{8,0},{12,4},{16,24},{20,28},{24,16},{28,20},{1,9},{5... | collective-permute-start | bytes 1032200 | tf_op jit(solution)/shard_map/ppermute | solution.py:1214
  410.2 22.3 %collective-permute-start.18 = (bf16[112,1536]{1,0:T(8,128)(2,1)}, bf16[112,1536]{1,0:T(8,128)(2,1)S(1)}, u32[]{:S(2)}, u32[]{:S(2)}) collective-permute-start(bf16[112,1536]{1,0:T(8,128)(2,1)} %get-tuple-element.158), channel_id=1, source_target_pairs={{0,16},{4,20},{8,24},{12,28},{16,0},{20,4},{24,8},{28,12},{1,17},{... | collective-permute-start | bytes 1032200 | tf_op jit(solution)/shard_map/ppermute | solution.py:1214
  414.7 17.8 %collective-permute-start.19 = (bf16[112,1536]{1,0:T(8,128)(2,1)}, bf16[112,1536]{1,0:T(8,128)(2,1)S(1)}, u32[]{:S(2)}, u32[]{:S(2)}) collective-permute-start(bf16[112,1536]{1,0:T(8,128)(2,1)} %get-tuple-element.159), channel_id=1, source_target_pairs={{0,24},{4,28},{8,16},{12,20},{16,8},{20,12},{24,0},{28,4},{1,25},{... | collective-permute-start | bytes 1032200 | tf_op jit(solution)/shard_map/ppermute | solution.py:1214
  421.9 15.8 %collective-permute-start.27 = (bf16[96,384]{1,0:T(8,128)(2,1)}, bf16[96,384]{1,0:T(8,128)(2,1)S(1)}, u32[]{:S(2)}, u32[]{:S(2)}) collective-permute-start(bf16[96,384]{1,0:T(8,128)(2,1)} %get-tuple-element.182), channel_id=1, source_target_pairs={{0,1},{1,2},{2,3},{3,0},{4,5},{5,6},{6,7},{7,4},{8,9},{9,10},{10,1... | collective-permute-start | bytes 221192 | tf_op jit(solution)/shard_map/ppermute | solution.py:1211
  428.7 19.5 %collective-permute-start.28 = (bf16[96,384]{1,0:T(8,128)(2,1)S(1)}, bf16[96,384]{1,0:T(8,128)(2,1)S(1)}, u32[]{:S(2)}, u32[]{:S(2)}) collective-permute-start(bf16[96,384]{1,0:T(8,128)(2,1)S(1)} %copy-done.37), channel_id=1, source_target_pairs={{0,2},{1,3},{2,0},{3,1},{4,6},{5,7},{6,4},{7,5},{8,10},{9,11},{10,... | collective-permute-start | bytes 221192 | tf_op jit(solution)/shard_map/ppermute | solution.py:1211
  430.6 17.6 %collective-permute-start.29 = (bf16[96,384]{1,0:T(8,128)(2,1)S(1)}, bf16[96,384]{1,0:T(8,128)(2,1)S(1)}, u32[]{:S(2)}, u32[]{:S(2)}) collective-permute-start(bf16[96,384]{1,0:T(8,128)(2,1)S(1)} %copy-done.36), channel_id=1, source_target_pairs={{0,3},{1,0},{2,1},{3,2},{4,7},{5,4},{6,5},{7,6},{8,11},{9,8},{10,9... | collective-permute-start | bytes 221192 | tf_op jit(solution)/shard_map/ppermute | solution.py:1211
  (49 other events, 315.6 us)
Sparse Core Ops, SparseCore 0:
  31.7 45.0 all-gather.4
  88.4 64.3 all-gather.6
where the time goes:
time: 465 us; the launch traced here: 458 us
  Pallas kernels  222 us (48%)
  waiting for transfers between devices  127 us (27%)
  starting transfers between devices  55 us (12%)
  local copies, waits for them, and re-layouts  23.8 us (5%)
  between operations  15.3 us (3%)
  other arithmetic  15 us (3%)
    ppermute x3, waiting for transfers between devices, body(): received = lax.ppermute(dx, 'tensor', left[s - 1:])  65.3 us
    pallas_call x4, Pallas kernels, attend_back(): pl.pallas_call(kernel, grid_spec=pltpu.PrefetchScalarGridSpec(num_scalar_...  46.5 us
    pallas_call x1, Pallas kernels, middle_layer(): pl.pallas_call(partial(middle_kernel, nt), grid=(ROWS // BLOCK,), in_spec...  41 us
    all_gather x1, waiting for transfers between devices, body(): mine = lax.all_gather(around, 'dp', axis=0)  36 us
    pallas_call x4, Pallas kernels, project(): pl.pallas_call(project_kernel, out_shape=(jax.ShapeDtypeStruct((ROWS, D),...  25.2 us
    ppermute x9, starting transfers between devices, over_tensor(): lax.ppermute(parts[s], 'tensor', ring(nt, s))  23.1 us
    pallas_call x2, Pallas kernels, attn_outer(): pl.pallas_call(kernel, grid_spec=pltpu.PrefetchScalarGridSpec(num_scalar_...  20.2 us
    pallas_call x1, Pallas kernels, attend(): pl.pallas_call(attend_kernel, grid_spec=pltpu.PrefetchScalarGridSpec(num_...  17.5 us
  transfers between devices with their start and end apart: 35, of which 6 were waited for; matrix products, arithmetic and copies ran while one was open for 6% of the time, Pallas kernels for 30%

commit v1 on v0

--- a/solution.py
+++ b/solution.py
@@ -92,7 +92,8 @@
     )(x)
 
 
-def project_kernel(x_ref, vec_ref, w_ref, n_ref, o_ref):
+def project_kernel(x_ref, vec_ref, w_ref, *refs):
+    n_ref, o_ref = refs[-2:]
     hat, _ = normalize(x_ref[...].astype(F32))
     normed = (hat * replicated(vec_ref, FG)).astype(BF)
     n_ref[...] = normed
@@ -104,7 +105,7 @@
     o_ref[:, n - D :] = (dot(normed, w_ref[:, n - D :]) + by_head(vec_ref, VB)).astype(BF)
 
 
-def project(x, vec, w):
+def project(x, vec, w, *first):
     n = w.shape[1]
     return pl.pallas_call(
         project_kernel,
@@ -117,6 +118,7 @@
             pl.BlockSpec((TILE, D), lambda i: (i, 0)),
             pl.BlockSpec(vec.shape, lambda i: (0, 0)),
             pl.BlockSpec((D, n), lambda i: (0, 0), pipeline_mode=pl.Buffered(1)),
+            *[HERE] * len(first),
         ],
         out_specs=(
             pl.BlockSpec((TILE, D), lambda i: (i, 0)),
@@ -126,7 +128,7 @@
             flops=2 * ROWS * D * n, bytes_accessed=2 * D * n + 2 * ROWS * (2 * D + n), transcendentals=0
         ),
         name="project",
-    )(x, vec, w)
+    )(x, vec, w, *first)
 
 
 def token_info(shard):
@@ -673,14 +675,17 @@
             out_refs[1][...] = value[:, 1 - i]
 
 
-def ffn_outer_kernel(core_ref, n2_ref, pg_ref, g_ref, hn_ref, *out_refs):
-    @pl.when(pl.program_id(0) == 0)
-    def _():
-        put(core_ref[0], out_refs, tn(n2_ref[...], pg_ref[...]))
-
-    @pl.when(pl.program_id(0) == 1)
-    def _():
-        put(core_ref[0], out_refs, tn(g_ref[...], hn_ref[...]))
+def ffn_outer_kernel(core_ref, n2_ref, pg_ref, g_ref, hn_ref, *refs):
+    out_refs, turned_ref = refs[:-1], refs[-1]
+    for j, (left, right) in enumerate(((n2_ref, pg_ref), (g_ref, hn_ref))):
+
+        @pl.when(pl.program_id(0) == j)
+        def _(left=left, right=right):
+            @pl.when(pl.program_id(1) == 0)
+            def _():
+                turned_ref[...] = left[...].T
+
+            put(core_ref[0], out_refs, dot(turned_ref[...], right[...]))
 
 
 def ffn_outer(core, nt, nb, outs, n2, pg, g, hn):
@@ -698,6 +703,7 @@
                 pl.BlockSpec((ROWS, f), lambda j, i, c: (0, i * j)),
             ],
             out_specs=(pl.BlockSpec((nb // outs, None, None, r, f), lambda j, i, c: (0, i, j, 0, 0)),) * outs,
+            scratch_shapes=[pltpu.VMEM((D, ROWS), BF)],
         ),
         out_shape=(jax.ShapeDtypeStruct((nb // outs, nt, 2, r, f), BF),) * outs,
         cost_estimate=pl.CostEstimate(
@@ -707,14 +713,21 @@
     )(core, n2, pg, g, hn)
 
 
-def attn_outer_kernel(terms, core_ref, ins, outs):
+def attn_outer_kernel(terms, again, core_ref, ins, outs, turned_ref):
     for m, pairs in enumerate(terms):
 
         @pl.when(pl.program_id(0) == m)
-        def _(pairs=pairs):
-            total = tn(ins[pairs[0][0]][...], ins[pairs[0][1]][...])
-            for a, b in pairs[1:]:
-                total += tn(ins[a][...], ins[b][...])
+        def _(m=m, pairs=pairs):
+            total = None
+            for a, b in pairs:
+                if m and a in again:
+                    left = turned_ref[again.index(a)]
+                else:
+                    left = ins[a][...].T
+                    if a in again:
+                        turned_ref[again.index(a)] = left
+                part = dot(left, ins[b][...])
+                total = part if total is None else total + part
             put(core_ref[0], outs, total)
 
 
@@ -727,8 +740,11 @@
     terms = [[(where[id(u)], where[id(v)]) for u, v in m] for m in matrices]
     n = len(args)
 
+    lefts = [a for m in terms for a, _ in m]
+    again = sorted({a for a in lefts if lefts.count(a) > 1})
+
     def kernel(core_ref, *refs):
-        attn_outer_kernel(terms, core_ref, refs[:n], refs[n + len(first) :])
+        attn_outer_kernel(terms, again, core_ref, refs[:n], refs[n + len(first) : -1], refs[-1])
 
     r = D // nb
     whole = pl.BlockSpec((ROWS, D), lambda i, c: (0, 0), pipeline_mode=pl.Buffered(1))
@@ -740,6 +756,7 @@
             grid=(len(matrices),),
             in_specs=[whole] * n + [HERE] * len(first),
             out_specs=(pl.BlockSpec((nb // outs, r, D), lambda i, c: (0, 0, i)),) * outs,
+            scratch_shapes=[pltpu.VMEM((max(len(again), 1), D, ROWS), BF)],
         ),
         out_shape=(jax.ShapeDtypeStruct((nb // outs, r, len(matrices) * D), BF),) * outs,
         cost_estimate=pl.CostEstimate(
@@ -966,9 +983,8 @@
     )(dx, received, x, middle_grad, vec, layer_output)
 
 
-def around_kernel(rows, cols, t_ref, *refs):
-    ins, o_ref = refs[:-2], refs[-1]
-    nt = len(ins)
+def around_kernel(rows, cols, nt, t_ref, *refs):
+    ins, o_ref = refs[:nt], refs[-1]
     for t in range(nt):
 
         @pl.when(t_ref[0] == t)
@@ -981,19 +997,19 @@
                 o_ref[rows:, j * 4 * cols : (j + 1) * 4 * cols] = block[j][rows:]
 
 
-def assemble_around(tvec, rows, cols, blocks, first):
+def assemble_around(tvec, rows, cols, blocks, *first):
     nt, n = len(blocks), blocks[0].shape[0]
     return pl.pallas_call(
-        partial(around_kernel, rows, cols),
+        partial(around_kernel, rows, cols, nt),
         grid_spec=pltpu.PrefetchScalarGridSpec(
             num_scalar_prefetch=1,
             grid=(1,),
-            in_specs=[pl.BlockSpec(b.shape, lambda i, t: (0, 0)) for b in blocks] + [HERE],
+            in_specs=[pl.BlockSpec(b.shape, lambda i, t: (0, 0)) for b in blocks] + [HERE] * len(first),
             out_specs=pl.BlockSpec((n, 4 * D), lambda i, t: (0, 0)),
         ),
         out_shape=jax.ShapeDtypeStruct((n, 4 * D), BF),
         name="around",
-    )(tvec, *blocks, first)
+    )(tvec, *blocks, *first)
 
 
 def assemble_kernel(a_ref, qkv_ref, kv_ref, out_ref, small_ref):
@@ -1028,7 +1044,8 @@
     )(a)
 
 
-def pack_kernel(x_ref, up_ref, down_ref, _, o_ref, ffn_ref):
+def pack_kernel(x_ref, up_ref, down_ref, *refs):
+    o_ref, ffn_ref = refs[-2:]
     r = up_ref.shape[0]
     o_ref[:ROWS] = x_ref[...]
     for ref, at in ((o_ref, ROWS), (ffn_ref, 0)):
@@ -1036,14 +1053,14 @@
         ref[at + r : at + 2 * r] = down_ref[...]
 
 
-def pack(x, up, down_t, first):
+def pack(x, up, down_t, *first):
     r, f = up.shape
     return pl.pallas_call(
         pack_kernel,
-        in_specs=[pl.BlockSpec(memory_space=pltpu.VMEM)] * 3 + [HERE],
+        in_specs=[pl.BlockSpec(memory_space=pltpu.VMEM)] * 3 + [HERE] * len(first),
         out_shape=(jax.ShapeDtypeStruct((ROWS + 2 * r, f), BF), jax.ShapeDtypeStruct((2 * r, f), BF)),
         name="pack",
-    )(x, up, down_t, first)
+    )(x, up, down_t, *first)
 
 
 def order_kernel(t_ref, *refs):
@@ -1121,6 +1138,8 @@
     f = FF // nt
     layer_input = sort_rows(layer_input)
     output_grad = sort_rows(output_grad)
+    x = [layer_input, lax.ppermute(layer_input, "tensor", right)]
+    ak = jnp.stack([key_columns(t - s) for s in range(nt)])
 
     places = [QB, VB, IG, UB, HG, OB, DB, FG, SG]
     vectors = split + whole
@@ -1152,18 +1171,18 @@
         around = around[:, :rows].reshape(nt, rows, 4, cols).transpose(1, 2, 0, 3)
         around = jnp.concatenate([around.reshape(rows, 4 * D), small_z], 0)
     else:
-        around = assemble_around(tvec, rows, cols, around, layer_input)
+        around = assemble_around(tvec, rows, cols, around, x[1], output_grad, ak)
     mine = lax.all_gather(around, "dp", axis=0)
 
     if rows % 16:
         ffn = jnp.concatenate([up_weight, down_weight.T], 0)
-        both = jnp.concatenate([layer_input, ffn], 0)
+        both = jnp.concatenate([x[1], ffn], 0)
     else:
-        both, ffn = pack(layer_input, up_weight, down_weight.T, around)
+        both, ffn = pack(x[1], up_weight, down_weight.T, around)
     one = lax.ppermute(both, "tensor", ring(nt, 1))
     ffn = [both, one] + [lax.ppermute(ffn, "tensor", ring(nt, s)) for s in range(2, nt)]
-    x = [layer_input, one]
-    for s in range(2, nt):
+    x.append(one)
+    for s in range(3, nt):
         x.append(lax.ppermute(x[-1][:ROWS], "tensor", right[s - 1 :]))
     if rows % 16:
         w4, small = mine[:, :rows].reshape(D, 4 * D), mine[:, rows:]
@@ -1185,11 +1204,10 @@
     n0, own = project(x[0], vec, w_qkv)
     normed, others = [n0], []
     for s in range(1, nt):
-        ns, kv = project(x[s], vec, w_kv)
+        ns, kv = project(x[s], vec, w_kv, *([own] if s == nt - 1 else []))
         normed.append(ns)
         others.append(kv)
     aq = query_columns(t, offsets)
-    ak = jnp.stack([key_columns(t - s) for s in range(nt)])
     context, qq = attend(tvec, own, others, aq, ak)
 
     g = output_grad

time: 465 us -> 459 us (0.987)
  waiting for transfers between devices: 127 us -> 117 us
    ppermute x3, waiting for transfers between devices: 65.3 us -> 34.8 us  [body(): received = lax.ppermute(dx, 'tensor', left[s - 1:])]
    ppermute x0 -> x1, waiting for transfers between devices: none -> 19.1 us  [body(): x = [layer_input, lax.ppermute(layer_input, 'tensor', right)]]
    all_gather x1, waiting for transfers between devices: 0.02 us -> 8.72 us  [body(): ffn = lax.all_gather(ffn, 'dp', axis=0).reshape(n_dp, nt, 2, rows, f)]
    ppermute x3, waiting for transfers between devices: 6.55 us -> 0.01 us  [body(): lax.ppermute(mine, 'tensor', ring(nt, s))]
  transfers between devices with their start and end apart: 35 -> 35, of which waited for: 6 -> 7; matrix products, arithmetic and copies ran while one was open for 6% -> 6% of each run, Pallas kernels for 30% -> 31%
where the time goes in v1:
time: 459 us; the launch traced here: 452 us
  Pallas kernels  222 us (48%)
  waiting for transfers between devices  117 us (25%)
  starting transfers between devices  58.9 us (13%)
  local copies, waits for them, and re-layouts  23.5 us (5%)
  other arithmetic  16.3 us (4%)
  between operations  15.3 us (3%)
    pallas_call x4, Pallas kernels, attend_back(): pl.pallas_call(kernel, grid_spec=pltpu.PrefetchScalarGridSpec(num_scalar_...  46.5 us
    pallas_call x1, Pallas kernels, middle_layer(): pl.pallas_call(partial(middle_kernel, nt), grid=(ROWS // BLOCK,), in_spec...  41 us
    ppermute x3, waiting for transfers between devices, body(): received = lax.ppermute(dx, 'tensor', left[s - 1:])  34.8 us
    all_gather x1, waiting for transfers between devices, body(): mine = lax.all_gather(around, 'dp', axis=0)  34.4 us
    pallas_call x4, Pallas kernels, project(): pl.pallas_call(project_kernel, out_shape=(jax.ShapeDtypeStruct((ROWS, D),...  24.8 us
    ppermute x9, starting transfers between devices, over_tensor(): lax.ppermute(parts[s], 'tensor', ring(nt, s))  22 us
    pallas_call x2, Pallas kernels, attn_outer(): pl.pallas_call(kernel, grid_spec=pltpu.PrefetchScalarGridSpec(num_scalar_...  20 us
    ppermute x1, waiting for transfers between devices, body(): x = [layer_input, lax.ppermute(layer_input, 'tensor', right)]  19.1 us
  transfers between devices with their start and end apart: 35, of which 7 were waited for; matrix products, arithmetic and copies ran while one was open for 6% of the time, Pallas kernels for 31%

profile of v1, /device:TPU:0, one launch (start us, length us, event | category | flops | bytes accessed | tf_op | source)
XLA Modules:
  0.0 452.5 jit_solution(13191742535643103594)
XLA Ops:
  32.1 19.1 %collective-permute-done.3.refs_4_.x_ref.r_8_ = bf16[768,768]{1,0:T(8,128)(2,1)S(1)} collective-permute-done((bf16[768,768]{1,0:T(8,128)(2,1)}, bf16[768,768]{1,0:T(8,128)(2,1)S(1)}, u32[]{:S(2)}, u32[]{:S(2)}) %collective-permute-start.3) | collective-permute-done | bytes 1179680 | tf_op jit(solution)/shard_map/ppermute | solution.py:1141
  57.3 5.2 %collective-permute-start.4 = (bf16[960,768]{1,0:T(8,128)(2,1)}, bf16[960,768]{1,0:T(8,128)(2,1)S(1)}, u32[]{:S(2)}, u32[]{:S(2)}) collective-permute-start(bf16[960,768]{1,0:T(8,128)(2,1)} %get-tuple-element.115.refs_0_), channel_id=1, source_target_pairs={{0,1},{1,2},{2,3},{3,0},{4,5},{5,6},{6,7},{7,4},{8,9},{9,10},{10,1... | collective-permute-start | bytes 4423688 | tf_op jit(solution)/shard_map/ppermute | solution.py:1182
  67.2 34.4 %all-gather.5.cloned.1.call-done = bf16[896,3072]{1,0:T(8,128)(2,1)} async-done(((bf16[112,3072]{1,0:T(8,128)(2,1)}), bf16[896,3072]{1,0:T(8,128)(2,1)}) %all-gather.5.cloned.1.call-update) | async-done | bytes 5505040 | tf_op jit(solution)/shard_map/all_gather | solution.py:1175
  101.6 7.8 %assemble.1 = (bf16[768,2304]{1,0:T(8,128)(2,1)}, bf16[768,1536]{1,0:T(8,128)(2,1)}, bf16[768,768]{1,0:T(8,128)(2,1)}, bf16[8,16,3072]{2,1,0:T(8,128)(2,1)}) custom-call(bf16[8,112,3072]{2,1,0:T(8,128)(2,1)} %bitcast.35), custom_call_target="tpu_custom_call" | custom-call | tf_op jit(solution)/shard_map/assemble/pallas_call | solution.py:1029
  126.7 6.0 %project.5 = (bf16[768,768]{1,0:T(8,128)(2,1)}, bf16[768,1536]{1,0:T(8,128)(2,1)}) custom-call(bf16[768,768]{1,0:T(8,128)(2,1)} %copy-done.2, f32[4,5376]{1,0:T(4,128)} %maximum_convert_fusion.vec_ref, bf16[768,1536]{1,0:T(8,128)(2,1)} %get-tuple-element.113.w_ref.refs_4_.r_6_.r_7_), custom_call_target="tpu_custom_call" | custom-call | flops 1811939328 | bytes 7077888 | tf_op jit(solution)/shard_map/project/pallas_call | solution.py:110
  132.8 5.9 %project.6 = (bf16[768,768]{1,0:T(8,128)(2,1)}, bf16[768,1536]{1,0:T(8,128)(2,1)}) custom-call(bf16[960,768]{1,0:T(8,128)(2,1)} %copy-done, f32[4,5376]{1,0:T(4,128)} %maximum_convert_fusion.vec_ref, bf16[768,1536]{1,0:T(8,128)(2,1)} %get-tuple-element.113.w_ref.refs_4_.r_6_.r_7_), custom_call_target="tpu_custom_call" | custom-call | flops 1811939328 | bytes 7077888 | tf_op jit(solution)/shard_map/project/pallas_call | solution.py:110
  138.7 6.9 %project.4 = (bf16[768,768]{1,0:T(8,128)(2,1)}, bf16[768,2304]{1,0:T(8,128)(2,1)}) custom-call(bf16[768,768]{1,0:T(8,128)(2,1)} %sort_rows.2.x_ref.r_8_, f32[4,5376]{1,0:T(4,128)} %maximum_convert_fusion.vec_ref, bf16[768,2304]{1,0:T(8,128)(2,1)} %get-tuple-element.111.w_ref.r_7_), custom_call_target="tpu_custom_call" | custom-call | flops 2717908992 | bytes 9437184 | tf_op jit(solution)/shard_map/project/pallas_call | solution.py:110
  145.6 5.9 %project.7 = (bf16[768,768]{1,0:T(8,128)(2,1)}, bf16[768,1536]{1,0:T(8,128)(2,1)}) custom-call(bf16[768,768]{1,0:T(8,128)(2,1)} %collective-permute-done.5.x_ref.r_7_, f32[4,5376]{1,0:T(4,128)} %maximum_convert_fusion.vec_ref, bf16[768,1536]{1,0:T(8,128)(2,1)} %get-tuple-element.113.w_ref.refs_4_.r_6_.r_7_, ...), custom_call_target="tpu_custom_call" | custom-call | flops 1811939328 | bytes 7077888 | tf_op jit(solution)/shard_map/project/pallas_call | solution.py:110
  151.6 17.6 %attend.1 = (f32[768,768]{1,0:T(8,128)}, bf16[768,1536]{1,0:T(8,128)(2,1)}) custom-call(s32[1]{0:T(128)} %bitcast.t_ref.r_0_, bf16[768,2304]{1,0:T(8,128)(2,1)} %get-tuple-element.112.refs_0_.q_ref.refs_4_.r_3_.r_4_, bf16[768,768]{1,0:T(8,128)(2,1)} %copy.49.aq_ref, bf16[768,2304]{1,0:T(8,128)(2,1)} %get-tuple-element.112.refs_0_.q_ref.refs_4_.r_3_.r_4_, ...), custom_call_target="tpu_custom_call" | custom-call | flops 16000000000 | bytes 16777216 | tf_op jit(solution)/shard_map/attend/pallas_call | solution.py:327
  169.1 8.7 %all-gather.7.cloned.1.call-done = bf16[32,192,768]{2,1,0:T(8,128)(2,1)} async-done(((bf16[4,192,768]{2,1,0:T(8,128)(2,1)}), bf16[32,192,768]{2,1,0:T(8,128)(2,1)}) %all-gather.7.cloned.1.call-update) | async-done | bytes 9437200 | tf_op jit(solution)/shard_map/all_gather | solution.py:1196
  177.8 41.0 %middle.1 = (bf16[768,768]{1,0:T(8,128)(2,1)}, bf16[768,768]{1,0:T(8,128)(2,1)}, bf16[768,3072]{1,0:T(8,128)(2,1)}, bf16[768,3072]{1,0:T(8,128)(2,1)}, bf16[768,...) custom-call(f32[768,768]{1,0:T(8,128)} %get-tuple-element.119.c_ref,, ...), custom_call_target="tpu_custom_call" | custom-call | flops 16307453952 | bytes 31457280 | tf_op jit(solution)/shard_map/middle/pallas_call | solution.py:637
  218.8 15.6 %ffn_outer.1 = (bf16[4,4,2,96,768]{4,3,2,1,0:T(8,128)(2,1)}, bf16[4,4,2,96,768]{4,3,2,1,0:T(8,128)(2,1)}) custom-call(s32[1]{0:T(128)} %bitcast.14.core_ref, bf16[768,768]{1,0:T(8,128)(2,1)} %get-tuple-element.123.n2_ref, bf16[768,3072]{1,0:T(8,128)(2,1)} %get-tuple-element.124.pg_ref, bf16[768,768]{1,0:T(8,128)(2,1)} %sort_rows.3.refs_5_.g_ref, ...), custom_call_target="tpu_custom_call" | custom-call | flops 7247757312 | bytes 18874368 | tf_op jit(solution)/shard_map/ffn_outer/pallas_call | solution.py:694
  235.2 6.3 %attend_back.4 = (f32[768,768]{1,0:T(8,128)}, bf16[768,768]{1,0:T(8,128)(2,1)}, bf16[768,768]{1,0:T(8,128)(2,1)}, bf16[768,768]{1,0:T(8,128)(2,1)}, f32[8,768]{1,0:T(8,128)}) custom-call(s32[1]{0:T(128)} %bitcast.t_ref.r_0_, bf16[768,1536]{1,0:T(8,128)(2,1)} %get-tuple-element.118.r_1_, bf16[768,1536]{1,0:T(8,128)(2,1)} %get-tuple-element.122.r_2_, ...), custom_call_target="tpu_custom_call" | custom-call | flops 16000000000 | bytes 16777216 | tf_op jit(solution)/shard_map/attend_back/pallas_call | solution.py:471
  248.9 7.2 %halve.3 = (bf16[4,2,96,768]{3,2,1,0:T(8,128)(2,1)}, bf16[4,2,96,768]{3,2,1,0:T(8,128)(2,1)}, bf16[4,2,96,768]{3,2,1,0:T(8,128)(2,1)}, bf16[4,2,96,768]{3,2,1,0:T(8,128)(2,1)}) custom-call(s32[4]{0:T(128)} %iota_xor_fusion.order_ref, bf16[4,4,2,96,768]{4,3,2,1,0:T(8,128)(2,1)} %get-tuple-element.126.r_8_.refs_0_, ...), custom_call_target="tpu_custom_call" | custom-call | flops 2359296 | bytes 14155776 | tf_op jit(solution)/shard_map/halve/pallas_call | solution.py:800
  256.1 7.9 %attend_back.5 = (f32[768,768]{1,0:T(8,128)}, bf16[768,768]{1,0:T(8,128)(2,1)}, bf16[768,768]{1,0:T(8,128)(2,1)}, bf16[768,768]{1,0:T(8,128)(2,1)}, f32[8,768]{1,0:T(8,128)}) custom-call(s32[1]{0:T(128)} %bitcast.t_ref.r_0_, bf16[768,1536]{1,0:T(8,128)(2,1)} %get-tuple-element.118.r_1_, bf16[768,1536]{1,0:T(8,128)(2,1)} %get-tuple-element.122.r_2_, ...), custom_call_target="tpu_custom_call" | custom-call | flops 16000000000 | bytes 16777216 | tf_op jit(solution)/shard_map/attend_back/pallas_call | solution.py:471
  269.9 8.1 %attend_back.6 = (f32[768,768]{1,0:T(8,128)}, bf16[768,768]{1,0:T(8,128)(2,1)}, bf16[768,768]{1,0:T(8,128)(2,1)}, bf16[768,768]{1,0:T(8,128)(2,1)}, f32[8,768]{1,0:T(8,128)}) custom-call(s32[1]{0:T(128)} %bitcast.t_ref.r_0_, bf16[768,1536]{1,0:T(8,128)(2,1)} %get-tuple-element.118.r_1_, bf16[768,1536]{1,0:T(8,128)(2,1)} %get-tuple-element.122.r_2_, ...), custom_call_target="tpu_custom_call" | custom-call | flops 16000000000 | bytes 16777216 | tf_op jit(solution)/shard_map/attend_back/pallas_call | solution.py:471
  280.9 24.2 %attend_back.7 = (bf16[768,768]{1,0:T(8,128)(2,1)}, bf16[768,768]{1,0:T(8,128)(2,1)}, bf16[768,768]{1,0:T(8,128)(2,1)}, f32[768,768]{1,0:T(8,128)}, f32[8,768]{1,0:T(8,128)}) custom-call(s32[1]{0:T(128)} %bitcast.t_ref.r_0_, bf16[768,1536]{1,0:T(8,128)(2,1)} %get-tuple-element.118.r_1_, bf16[768,1536]{1,0:T(8,128)(2,1)} %get-tuple-element.122.r_2_, ...), custom_call_target="tpu_custom_call" | custom-call | flops 16000000000 | bytes 16777216 | tf_op jit(solution)/shard_map/attend_back/pallas_call | solution.py:471
  308.6 12.7 %collective-permute-done.13.refs_2_ = bf16[4,2,96,768]{3,2,1,0:T(8,128)(2,1)} collective-permute-done((bf16[4,2,96,768]{3,2,1,0:T(8,128)(2,1)}, bf16[4,2,96,768]{3,2,1,0:T(8,128)(2,1)}, u32[]{:S(2)}, u32[]{:S(2)}) %collective-permute-start.13) | collective-permute-done | bytes 1179680 | tf_op jit(solution)/shard_map/ppermute | solution.py:1232
  326.0 34.8 %collective-permute-done.11.r_ref.refs_4_ = bf16[768,768]{1,0:T(8,128)(2,1)} collective-permute-done((bf16[768,768]{1,0:T(8,128)(2,1)S(1)}, bf16[768,768]{1,0:T(8,128)(2,1)}, u32[]{:S(2)}, u32[]{:S(2)}) %collective-permute-start.11) | collective-permute-done | bytes 1179680 | tf_op jit(solution)/shard_map/ppermute | solution.py:1248
  360.8 5.9 %attn_outer.2 = (bf16[4,96,1536]{2,1,0:T(8,128)(2,1)}, bf16[4,96,1536]{2,1,0:T(8,128)(2,1)}) custom-call(s32[1]{0:T(128)} %bitcast.14.core_ref, bf16[768,768]{1,0:T(8,128)(2,1)} %get-tuple-element.140.refs_0_, bf16[768,768]{1,0:T(8,128)(2,1)} %get-tuple-element.141.refs_1_, bf16[768,768]{1,0:T(8,128)(2,1)} %get-tuple-element.142.refs_2_.refs_0_, ...), custom_call_target="tpu_custom_call" | custom-call | flops 1811939328 | bytes 4718592 | tf_op jit(solution)/shard_map/attn_outer/pallas_call | solution.py:752
  366.7 14.2 %attn_outer.3 = (bf16[4,96,1536]{2,1,0:T(8,128)(2,1)}, bf16[4,96,1536]{2,1,0:T(8,128)(2,1)}) custom-call(s32[1]{0:T(128)} %bitcast.14.core_ref, bf16[768,768]{1,0:T(8,128)(2,1)} %get-tuple-element.142.refs_2_.refs_0_, bf16[768,768]{1,0:T(8,128)(2,1)} %get-tuple-element.164.refs_1_, bf16[768,768]{1,0:T(8,128)(2,1)} %get-tuple-element.165.refs_2_, ...), custom_call_target="tpu_custom_call" | custom-call | flops 7247757312 | bytes 14155776 | tf_op jit(solution)/shard_map/attn_outer/pallas_call | solution.py:752
  381.4 6.3 %collective-permute-start.30 = (bf16[2,96,768]{2,1,0:T(8,128)(2,1)}, bf16[2,96,768]{2,1,0:T(8,128)(2,1)S(1)}, u32[]{:S(2)}, u32[]{:S(2)}) collective-permute-start(bf16[2,96,768]{2,1,0:T(8,128)(2,1)} %get-tuple-element.189), channel_id=1, source_target_pairs={{0,1},{1,2},{2,3},{3,0},{4,5},{5,6},{6,7},{7,4},{8,9},{9,10},{10,1... | collective-permute-start | bytes 884744 | tf_op jit(solution)/shard_map/ppermute | solution.py:1229
  395.9 3.9 collective-permute-start.31
  434.6 7.7 %finish.1 = (bf16[768,768]{1,0:T(8,128)(2,1)}, bf16[768,768]{1,0:T(8,128)(2,1)}) custom-call(f32[768,768]{1,0:T(8,128)} %get-tuple-element.135.dx_ref, bf16[768,768]{1,0:T(8,128)(2,1)} %collective-permute-done.11.r_ref.refs_4_, bf16[768,768]{1,0:T(8,128)(2,1)} %sort_rows.2.x_ref.r_8_, f32[768,768]{1,0:T(8,128)} %get-tuple-element.136.mg_ref, ...), custom_call_target="tpu_custom_call" | custom-call | flops 1811939328 | bytes 9437184 | tf_op jit(solution)/shard_map/finish/pallas_call | solution.py:973
  (277 shorter events, 123.9 us)
Async XLA Ops:
  7.2 94.4 %all-gather.5.cloned.1.call-start = ((), (), s32[]{:S(2)}) async-start(), calls=%async_computation | async-start | bytes 6193152 | tf_op jit(solution)/shard_map/all_gather | solution.py:1175
  11.7 20.4 %collective-permute-start = (bf16[112,768]{1,0:T(8,128)(2,1)S(1)}, bf16[112,768]{1,0:T(8,128)(2,1)S(1)}, u32[]{:S(2)}, u32[]{:S(2)}) collective-permute-start(bf16[112,768]{1,0:T(8,128)(2,1)S(1)} %fusion.20.refs_0_), channel_id=1, source_target_pairs={{0,1},{1,2},{2,3},{3,0},{4,5},{5,6},{6,7},{7,4},{8,9},{9,10},{10,1... | collective-permute-start | bytes 516104 | tf_op jit(solution)/shard_map/ppermute | solution.py:1167
  14.8 17.3 %collective-permute-start.1 = (bf16[112,768]{1,0:T(8,128)(2,1)S(1)}, bf16[112,768]{1,0:T(8,128)(2,1)S(1)}, u32[]{:S(2)}, u32[]{:S(2)}) collective-permute-start(bf16[112,768]{1,0:T(8,128)(2,1)S(1)} %fusion.20.refs_0_), channel_id=1, source_target_pairs={{0,2},{1,3},{2,0},{3,1},{4,6},{5,7},{6,4},{7,5},{8,10},{9,11},{10,... | collective-permute-start | bytes 516104 | tf_op jit(solution)/shard_map/ppermute | solution.py:1167
  22.1 29.1 %collective-permute-start.3 = (bf16[768,768]{1,0:T(8,128)(2,1)}, bf16[768,768]{1,0:T(8,128)(2,1)S(1)}, u32[]{:S(2)}, u32[]{:S(2)}) collective-permute-start(bf16[768,768]{1,0:T(8,128)(2,1)} %sort_rows.2.x_ref.r_8_), channel_id=1, source_target_pairs={{0,1},{1,2},{2,3},{4,5},{5,6},{6,7},{8,9},{9,10},{10,11},{12,13},{... | collective-permute-start | bytes 3538952 | tf_op jit(solution)/shard_map/ppermute | solution.py:1141
  54.5 123.3 %all-gather.7.cloned.1.call-start = ((), (), s32[]{:S(2)}) async-start(), calls=%async_computation.1 | async-start | bytes 10616832 | tf_op jit(solution)/shard_map/all_gather | solution.py:1196
  57.3 52.2 %collective-permute-start.4 = (bf16[960,768]{1,0:T(8,128)(2,1)}, bf16[960,768]{1,0:T(8,128)(2,1)S(1)}, u32[]{:S(2)}, u32[]{:S(2)}) collective-permute-start(bf16[960,768]{1,0:T(8,128)(2,1)} %get-tuple-element.115.refs_0_), channel_id=1, source_target_pairs={{0,1},{1,2},{2,3},{3,0},{4,5},{5,6},{6,7},{7,4},{8,9},{9,10},{10,1... | collective-permute-start | bytes 4423688 | tf_op jit(solution)/shard_map/ppermute | solution.py:1182
  62.5 46.9 %collective-permute-start.6 = (bf16[192,768]{1,0:T(8,128)(2,1)}, bf16[192,768]{1,0:T(8,128)(2,1)S(1)}, u32[]{:S(2)}, u32[]{:S(2)}) collective-permute-start(bf16[192,768]{1,0:T(8,128)(2,1)} %get-tuple-element.121), channel_id=1, source_target_pairs={{0,2},{1,3},{2,0},{3,1},{4,6},{5,7},{6,4},{7,5},{8,10},{9,11},{10,... | collective-permute-start | bytes 884744 | tf_op jit(solution)/shard_map/ppermute | solution.py:1183
  64.4 44.9 %collective-permute-start.7 = (bf16[192,768]{1,0:T(8,128)(2,1)}, bf16[192,768]{1,0:T(8,128)(2,1)S(1)}, u32[]{:S(2)}, u32[]{:S(2)}) collective-permute-start(bf16[192,768]{1,0:T(8,128)(2,1)} %get-tuple-element.121), channel_id=1, source_target_pairs={{0,3},{1,0},{2,1},{3,2},{4,7},{5,4},{6,5},{7,6},{8,11},{9,8},{10,9... | collective-permute-start | bytes 884744 | tf_op jit(solution)/shard_map/ppermute | solution.py:1183
  114.8 30.8 %collective-permute-start.5 = (bf16[768,768]{1,0:T(8,128)(2,1)S(1)}, bf16[768,768]{1,0:T(8,128)(2,1)}, u32[]{:S(2)}, u32[]{:S(2)}) collective-permute-start(bf16[768,768]{1,0:T(8,128)(2,1)S(1)} %slice.79), channel_id=1, source_target_pairs={{2,3},{6,7},{10,11},{14,15},{18,19},{22,23},{26,27},{30,31}} | collective-permute-start | bytes 3538952 | tf_op jit(solution)/shard_map/ppermute | solution.py:1186
  241.5 22.5 %collective-permute-start.9 = (bf16[768,768]{1,0:T(8,128)(2,1)}, bf16[768,768]{1,0:T(8,128)(2,1)S(1)}, u32[]{:S(2)}, u32[]{:S(2)}) collective-permute-start(bf16[768,768]{1,0:T(8,128)(2,1)} %get-tuple-element.132), channel_id=1, source_target_pairs={{3,2},{7,6},{11,10},{15,14},{19,18},{23,22},{27,26},{31,30}} | collective-permute-start | bytes 3538952 | tf_op jit(solution)/shard_map/ppermute | solution.py:1248
  266.3 42.3 %collective-permute-start.12 = (bf16[4,2,96,768]{3,2,1,0:T(8,128)(2,1)}, bf16[4,2,96,768]{3,2,1,0:T(8,128)(2,1)}, u32[]{:S(2)}, u32[]{:S(2)}) collective-permute-start(bf16[4,2,96,768]{3,2,1,0:T(8,128)(2,1)} %get-tuple-element.144), channel_id=1, source_target_pairs={{0,8},{4,12},{8,0},{12,4},{16,24},{20,28},{24,16},{28,20},{1,9},{5... | collective-permute-start | bytes 3538952 | tf_op jit(solution)/shard_map/ppermute | solution.py:1232
  267.9 53.5 %collective-permute-start.13 = (bf16[4,2,96,768]{3,2,1,0:T(8,128)(2,1)}, bf16[4,2,96,768]{3,2,1,0:T(8,128)(2,1)}, u32[]{:S(2)}, u32[]{:S(2)}) collective-permute-start(bf16[4,2,96,768]{3,2,1,0:T(8,128)(2,1)} %get-tuple-element.145), channel_id=1, source_target_pairs={{0,16},{4,20},{8,24},{12,28},{16,0},{20,4},{24,8},{28,12},{1,17},{... | collective-permute-start | bytes 3538952 | tf_op jit(solution)/shard_map/ppermute | solution.py:1232
  268.4 52.9 %collective-permute-start.14 = (bf16[4,2,96,768]{3,2,1,0:T(8,128)(2,1)}, bf16[4,2,96,768]{3,2,1,0:T(8,128)(2,1)}, u32[]{:S(2)}, u32[]{:S(2)}) collective-permute-start(bf16[4,2,96,768]{3,2,1,0:T(8,128)(2,1)} %get-tuple-element.146), channel_id=1, source_target_pairs={{0,24},{4,28},{8,16},{12,20},{16,8},{20,12},{24,0},{28,4},{1,25},{... | collective-permute-start | bytes 3538952 | tf_op jit(solution)/shard_map/ppermute | solution.py:1232
  279.6 81.2 %collective-permute-start.11 = (bf16[768,768]{1,0:T(8,128)(2,1)S(1)}, bf16[768,768]{1,0:T(8,128)(2,1)}, u32[]{:S(2)}, u32[]{:S(2)}) collective-permute-start(bf16[768,768]{1,0:T(8,128)(2,1)S(1)} %add_convert_fusion.r_9_), channel_id=1, source_target_pairs={{1,0},{2,1},{3,2},{5,4},{6,5},{7,6},{9,8},{10,9},{11,10},{13,12},{... | collective-permute-start | bytes 3538952 | tf_op jit(solution)/shard_map/ppermute | solution.py:1248
  381.4 21.8 %collective-permute-start.30 = (bf16[2,96,768]{2,1,0:T(8,128)(2,1)}, bf16[2,96,768]{2,1,0:T(8,128)(2,1)S(1)}, u32[]{:S(2)}, u32[]{:S(2)}) collective-permute-start(bf16[2,96,768]{2,1,0:T(8,128)(2,1)} %get-tuple-element.189), channel_id=1, source_target_pairs={{0,1},{1,2},{2,3},{3,0},{4,5},{5,6},{6,7},{7,4},{8,9},{9,10},{10,1... | collective-permute-start | bytes 884744 | tf_op jit(solution)/shard_map/ppermute | solution.py:1229
  393.6 15.6 %collective-permute-start.25 = (bf16[96,1536]{1,0:T(8,128)(2,1)}, bf16[96,1536]{1,0:T(8,128)(2,1)S(1)}, u32[]{:S(2)}, u32[]{:S(2)}) collective-permute-start(bf16[96,1536]{1,0:T(8,128)(2,1)} %get-tuple-element.179), channel_id=1, source_target_pairs={{0,16},{4,20},{8,24},{12,28},{16,0},{20,4},{24,8},{28,12},{1,17},{... | collective-permute-start | bytes 884744 | tf_op jit(solution)/shard_map/ppermute | solution.py:1232
  395.2 15.4 %collective-permute-start.26 = (bf16[96,1536]{1,0:T(8,128)(2,1)}, bf16[96,1536]{1,0:T(8,128)(2,1)}, u32[]{:S(2)}, u32[]{:S(2)}) collective-permute-start(bf16[96,1536]{1,0:T(8,128)(2,1)} %get-tuple-element.180), channel_id=1, source_target_pairs={{0,24},{4,28},{8,16},{12,20},{16,8},{20,12},{24,0},{28,4},{1,25},{... | collective-permute-start | bytes 884744 | tf_op jit(solution)/shard_map/ppermute | solution.py:1232
  395.9 20.4 %collective-permute-start.31 = (bf16[2,96,768]{2,1,0:T(8,128)(2,1)}, bf16[2,96,768]{2,1,0:T(8,128)(2,1)S(1)}, u32[]{:S(2)}, u32[]{:S(2)}) collective-permute-start(bf16[2,96,768]{2,1,0:T(8,128)(2,1)} %get-tuple-element.190), channel_id=1, source_target_pairs={{0,2},{1,3},{2,0},{3,1},{4,6},{5,7},{6,4},{7,5},{8,10},{9,11},{10,... | collective-permute-start | bytes 884744 | tf_op jit(solution)/shard_map/ppermute | solution.py:1229
  403.2 22.0 %collective-permute-start.17 = (bf16[112,1536]{1,0:T(8,128)(2,1)}, bf16[112,1536]{1,0:T(8,128)(2,1)S(1)}, u32[]{:S(2)}, u32[]{:S(2)}) collective-permute-start(bf16[112,1536]{1,0:T(8,128)(2,1)} %get-tuple-element.157), channel_id=1, source_target_pairs={{0,8},{4,12},{8,0},{12,4},{16,24},{20,28},{24,16},{28,20},{1,9},{5... | collective-permute-start | bytes 1032200 | tf_op jit(solution)/shard_map/ppermute | solution.py:1232
  404.6 22.0 %collective-permute-start.18 = (bf16[112,1536]{1,0:T(8,128)(2,1)}, bf16[112,1536]{1,0:T(8,128)(2,1)S(1)}, u32[]{:S(2)}, u32[]{:S(2)}) collective-permute-start(bf16[112,1536]{1,0:T(8,128)(2,1)} %get-tuple-element.158), channel_id=1, source_target_pairs={{0,16},{4,20},{8,24},{12,28},{16,0},{20,4},{24,8},{28,12},{1,17},{... | collective-permute-start | bytes 1032200 | tf_op jit(solution)/shard_map/ppermute | solution.py:1232
  409.3 17.3 %collective-permute-start.19 = (bf16[112,1536]{1,0:T(8,128)(2,1)}, bf16[112,1536]{1,0:T(8,128)(2,1)S(1)}, u32[]{:S(2)}, u32[]{:S(2)}) collective-permute-start(bf16[112,1536]{1,0:T(8,128)(2,1)} %get-tuple-element.159), channel_id=1, source_target_pairs={{0,24},{4,28},{8,16},{12,20},{16,8},{20,12},{24,0},{28,4},{1,25},{... | collective-permute-start | bytes 1032200 | tf_op jit(solution)/shard_map/ppermute | solution.py:1232
  416.3 15.4 %collective-permute-start.27 = (bf16[96,384]{1,0:T(8,128)(2,1)}, bf16[96,384]{1,0:T(8,128)(2,1)S(1)}, u32[]{:S(2)}, u32[]{:S(2)}) collective-permute-start(bf16[96,384]{1,0:T(8,128)(2,1)} %get-tuple-element.182), channel_id=1, source_target_pairs={{0,1},{1,2},{2,3},{3,0},{4,5},{5,6},{6,7},{7,4},{8,9},{9,10},{10,1... | collective-permute-start | bytes 221192 | tf_op jit(solution)/shard_map/ppermute | solution.py:1229
  423.1 19.2 %collective-permute-start.28 = (bf16[96,384]{1,0:T(8,128)(2,1)S(1)}, bf16[96,384]{1,0:T(8,128)(2,1)S(1)}, u32[]{:S(2)}, u32[]{:S(2)}) collective-permute-start(bf16[96,384]{1,0:T(8,128)(2,1)S(1)} %copy-done.42), channel_id=1, source_target_pairs={{0,2},{1,3},{2,0},{3,1},{4,6},{5,7},{6,4},{7,5},{8,10},{9,11},{10,... | collective-permute-start | bytes 221192 | tf_op jit(solution)/shard_map/ppermute | solution.py:1229
  425.2 17.1 %collective-permute-start.29 = (bf16[96,384]{1,0:T(8,128)(2,1)S(1)}, bf16[96,384]{1,0:T(8,128)(2,1)S(1)}, u32[]{:S(2)}, u32[]{:S(2)}) collective-permute-start(bf16[96,384]{1,0:T(8,128)(2,1)S(1)} %copy-done.41), channel_id=1, source_target_pairs={{0,3},{1,0},{2,1},{3,2},{4,7},{5,4},{6,5},{7,6},{8,11},{9,8},{10,9... | collective-permute-start | bytes 221192 | tf_op jit(solution)/shard_map/ppermute | solution.py:1229
  (54 other events, 389.0 us)
Sparse Core Ops, SparseCore 0:
  54.6 46.9 all-gather.4
  113.2 64.6 all-gather.6

commit v2 on v1

--- a/solution.py
+++ b/solution.py
@@ -113,16 +113,16 @@
             jax.ShapeDtypeStruct((ROWS, D), BF),
             jax.ShapeDtypeStruct((ROWS, n), BF),
         ),
-        grid=(ROWS // TILE,),
+        grid=(ROWS // HALF,),
         in_specs=[
-            pl.BlockSpec((TILE, D), lambda i: (i, 0)),
+            pl.BlockSpec((HALF, D), lambda i: (i, 0)),
             pl.BlockSpec(vec.shape, lambda i: (0, 0)),
             pl.BlockSpec((D, n), lambda i: (0, 0), pipeline_mode=pl.Buffered(1)),
             *[HERE] * len(first),
         ],
         out_specs=(
-            pl.BlockSpec((TILE, D), lambda i: (i, 0)),
-            pl.BlockSpec((TILE, n), lambda i: (i, 0)),
+            pl.BlockSpec((HALF, D), lambda i: (i, 0)),
+            pl.BlockSpec((HALF, n), lambda i: (i, 0)),
         ),
         cost_estimate=pl.CostEstimate(
             flops=2 * ROWS * D * n, bytes_accessed=2 * D * n + 2 * ROWS * (2 * D + n), transcendentals=0

time: 459 us -> 457 us (level)
  transfers between devices with their start and end apart: 35 -> 35, of which waited for: 7 -> 7; matrix products, arithmetic and copies ran while one was open for 6% -> 6% of each run, Pallas kernels for 31% -> 30%
where the time goes in v2:
time: 457 us; the launch traced here: 451 us
  Pallas kernels  220 us (48%)
  waiting for transfers between devices  117 us (26%)
  starting transfers between devices  58.5 us (13%)
  local copies, waits for them, and re-layouts  23.4 us (5%)
  other arithmetic  16.3 us (4%)
  between operations  15.3 us (3%)
    pallas_call x4, Pallas kernels, attend_back(): pl.pallas_call(kernel, grid_spec=pltpu.PrefetchScalarGridSpec(num_scalar_...  46.5 us
    pallas_call x1, Pallas kernels, middle_layer(): pl.pallas_call(partial(middle_kernel, nt), grid=(ROWS // BLOCK,), in_spec...  41 us
    all_gather x1, waiting for transfers between devices, body(): mine = lax.all_gather(around, 'dp', axis=0)  34.4 us
    ppermute x3, waiting for transfers between devices, body(): received = lax.ppermute(dx, 'tensor', left[s - 1:])  33.6 us
    pallas_call x4, Pallas kernels, project(): pl.pallas_call(project_kernel, out_shape=(jax.ShapeDtypeStruct((ROWS, D),...  23.5 us
    ppermute x9, starting transfers between devices, over_tensor(): lax.ppermute(parts[s], 'tensor', ring(nt, s))  22 us
    pallas_call x2, Pallas kernels, attn_outer(): pl.pallas_call(kernel, grid_spec=pltpu.PrefetchScalarGridSpec(num_scalar_...  20 us
    ppermute x1, waiting for transfers between devices, body(): x = [layer_input, lax.ppermute(layer_input, 'tensor', right)]  19.1 us
  transfers between devices with their start and end apart: 35, of which 7 were waited for; matrix products, arithmetic and copies ran while one was open for 6% of the time, Pallas kernels for 30%

profile of v2, /device:TPU:0, one launch (start us, length us, event | category | flops | bytes accessed | tf_op | source)
XLA Modules:
  0.0 451.1 jit_solution(7084330050009174752)
XLA Ops:
  32.1 19.1 %collective-permute-done.3.refs_4_.x_ref.r_8_ = bf16[768,768]{1,0:T(8,128)(2,1)S(1)} collective-permute-done((bf16[768,768]{1,0:T(8,128)(2,1)}, bf16[768,768]{1,0:T(8,128)(2,1)S(1)}, u32[]{:S(2)}, u32[]{:S(2)}) %collective-permute-start.3) | collective-permute-done | bytes 1179680 | tf_op jit(solution)/shard_map/ppermute | solution.py:1141
  57.3 5.2 %collective-permute-start.4 = (bf16[960,768]{1,0:T(8,128)(2,1)}, bf16[960,768]{1,0:T(8,128)(2,1)S(1)}, u32[]{:S(2)}, u32[]{:S(2)}) collective-permute-start(bf16[960,768]{1,0:T(8,128)(2,1)} %get-tuple-element.115.refs_0_), channel_id=1, source_target_pairs={{0,1},{1,2},{2,3},{3,0},{4,5},{5,6},{6,7},{7,4},{8,9},{9,10},{10,1... | collective-permute-start | bytes 4423688 | tf_op jit(solution)/shard_map/ppermute | solution.py:1182
  67.2 34.4 %all-gather.5.cloned.1.call-done = bf16[896,3072]{1,0:T(8,128)(2,1)} async-done(((bf16[112,3072]{1,0:T(8,128)(2,1)}), bf16[896,3072]{1,0:T(8,128)(2,1)}) %all-gather.5.cloned.1.call-update) | async-done | bytes 5505040 | tf_op jit(solution)/shard_map/all_gather | solution.py:1175
  101.6 7.8 %assemble.1 = (bf16[768,2304]{1,0:T(8,128)(2,1)}, bf16[768,1536]{1,0:T(8,128)(2,1)}, bf16[768,768]{1,0:T(8,128)(2,1)}, bf16[8,16,3072]{2,1,0:T(8,128)(2,1)}) custom-call(bf16[8,112,3072]{2,1,0:T(8,128)(2,1)} %bitcast.35), custom_call_target="tpu_custom_call" | custom-call | tf_op jit(solution)/shard_map/assemble/pallas_call | solution.py:1029
  126.7 5.6 %project.5 = (bf16[768,768]{1,0:T(8,128)(2,1)}, bf16[768,1536]{1,0:T(8,128)(2,1)}) custom-call(bf16[768,768]{1,0:T(8,128)(2,1)} %copy-done.2, f32[4,5376]{1,0:T(4,128)} %maximum_convert_fusion.vec_ref, bf16[768,1536]{1,0:T(8,128)(2,1)} %get-tuple-element.113.w_ref.refs_4_.r_6_.r_7_), custom_call_target="tpu_custom_call" | custom-call | flops 1811939328 | bytes 7077888 | tf_op jit(solution)/shard_map/project/pallas_call | solution.py:110
  132.4 5.5 %project.6 = (bf16[768,768]{1,0:T(8,128)(2,1)}, bf16[768,1536]{1,0:T(8,128)(2,1)}) custom-call(bf16[960,768]{1,0:T(8,128)(2,1)} %copy-done, f32[4,5376]{1,0:T(4,128)} %maximum_convert_fusion.vec_ref, bf16[768,1536]{1,0:T(8,128)(2,1)} %get-tuple-element.113.w_ref.refs_4_.r_6_.r_7_), custom_call_target="tpu_custom_call" | custom-call | flops 1811939328 | bytes 7077888 | tf_op jit(solution)/shard_map/project/pallas_call | solution.py:110
  137.8 7.0 %project.4 = (bf16[768,768]{1,0:T(8,128)(2,1)}, bf16[768,2304]{1,0:T(8,128)(2,1)}) custom-call(bf16[768,768]{1,0:T(8,128)(2,1)} %sort_rows.2.x_ref.r_8_, f32[4,5376]{1,0:T(4,128)} %maximum_convert_fusion.vec_ref, bf16[768,2304]{1,0:T(8,128)(2,1)} %get-tuple-element.111.w_ref.r_7_), custom_call_target="tpu_custom_call" | custom-call | flops 2717908992 | bytes 9437184 | tf_op jit(solution)/shard_map/project/pallas_call | solution.py:110
  144.8 5.5 %project.7 = (bf16[768,768]{1,0:T(8,128)(2,1)}, bf16[768,1536]{1,0:T(8,128)(2,1)}) custom-call(bf16[768,768]{1,0:T(8,128)(2,1)} %collective-permute-done.5.x_ref.r_7_, f32[4,5376]{1,0:T(4,128)} %maximum_convert_fusion.vec_ref, bf16[768,1536]{1,0:T(8,128)(2,1)} %get-tuple-element.113.w_ref.refs_4_.r_6_.r_7_, ...), custom_call_target="tpu_custom_call" | custom-call | flops 1811939328 | bytes 7077888 | tf_op jit(solution)/shard_map/project/pallas_call | solution.py:110
  150.3 17.6 %attend.1 = (f32[768,768]{1,0:T(8,128)}, bf16[768,1536]{1,0:T(8,128)(2,1)}) custom-call(s32[1]{0:T(128)} %bitcast.t_ref.r_0_, bf16[768,2304]{1,0:T(8,128)(2,1)} %get-tuple-element.112.refs_0_.q_ref.refs_4_.r_3_.r_4_, bf16[768,768]{1,0:T(8,128)(2,1)} %copy.49.aq_ref, bf16[768,2304]{1,0:T(8,128)(2,1)} %get-tuple-element.112.refs_0_.q_ref.refs_4_.r_3_.r_4_, ...), custom_call_target="tpu_custom_call" | custom-call | flops 16000000000 | bytes 16777216 | tf_op jit(solution)/shard_map/attend/pallas_call | solution.py:327
  167.8 10.0 %all-gather.7.cloned.1.call-done = bf16[32,192,768]{2,1,0:T(8,128)(2,1)} async-done(((bf16[4,192,768]{2,1,0:T(8,128)(2,1)}), bf16[32,192,768]{2,1,0:T(8,128)(2,1)}) %all-gather.7.cloned.1.call-update) | async-done | bytes 9437200 | tf_op jit(solution)/shard_map/all_gather | solution.py:1196
  177.8 41.0 %middle.1 = (bf16[768,768]{1,0:T(8,128)(2,1)}, bf16[768,768]{1,0:T(8,128)(2,1)}, bf16[768,3072]{1,0:T(8,128)(2,1)}, bf16[768,3072]{1,0:T(8,128)(2,1)}, bf16[768,...) custom-call(f32[768,768]{1,0:T(8,128)} %get-tuple-element.119.c_ref,, ...), custom_call_target="tpu_custom_call" | custom-call | flops 16307453952 | bytes 31457280 | tf_op jit(solution)/shard_map/middle/pallas_call | solution.py:637
  218.8 15.6 %ffn_outer.1 = (bf16[4,4,2,96,768]{4,3,2,1,0:T(8,128)(2,1)}, bf16[4,4,2,96,768]{4,3,2,1,0:T(8,128)(2,1)}) custom-call(s32[1]{0:T(128)} %bitcast.14.core_ref, bf16[768,768]{1,0:T(8,128)(2,1)} %get-tuple-element.123.n2_ref, bf16[768,3072]{1,0:T(8,128)(2,1)} %get-tuple-element.124.pg_ref, bf16[768,768]{1,0:T(8,128)(2,1)} %sort_rows.3.refs_5_.g_ref, ...), custom_call_target="tpu_custom_call" | custom-call | flops 7247757312 | bytes 18874368 | tf_op jit(solution)/shard_map/ffn_outer/pallas_call | solution.py:694
  235.2 6.3 %attend_back.4 = (f32[768,768]{1,0:T(8,128)}, bf16[768,768]{1,0:T(8,128)(2,1)}, bf16[768,768]{1,0:T(8,128)(2,1)}, bf16[768,768]{1,0:T(8,128)(2,1)}, f32[8,768]{1,0:T(8,128)}) custom-call(s32[1]{0:T(128)} %bitcast.t_ref.r_0_, bf16[768,1536]{1,0:T(8,128)(2,1)} %get-tuple-element.118.r_1_, bf16[768,1536]{1,0:T(8,128)(2,1)} %get-tuple-element.122.r_2_, ...), custom_call_target="tpu_custom_call" | custom-call | flops 16000000000 | bytes 16777216 | tf_op jit(solution)/shard_map/attend_back/pallas_call | solution.py:471
  248.9 7.2 %halve.3 = (bf16[4,2,96,768]{3,2,1,0:T(8,128)(2,1)}, bf16[4,2,96,768]{3,2,1,0:T(8,128)(2,1)}, bf16[4,2,96,768]{3,2,1,0:T(8,128)(2,1)}, bf16[4,2,96,768]{3,2,1,0:T(8,128)(2,1)}) custom-call(s32[4]{0:T(128)} %iota_xor_fusion.order_ref, bf16[4,4,2,96,768]{4,3,2,1,0:T(8,128)(2,1)} %get-tuple-element.126.r_8_.refs_0_, ...), custom_call_target="tpu_custom_call" | custom-call | flops 2359296 | bytes 14155776 | tf_op jit(solution)/shard_map/halve/pallas_call | solution.py:800
  256.1 7.9 %attend_back.5 = (f32[768,768]{1,0:T(8,128)}, bf16[768,768]{1,0:T(8,128)(2,1)}, bf16[768,768]{1,0:T(8,128)(2,1)}, bf16[768,768]{1,0:T(8,128)(2,1)}, f32[8,768]{1,0:T(8,128)}) custom-call(s32[1]{0:T(128)} %bitcast.t_ref.r_0_, bf16[768,1536]{1,0:T(8,128)(2,1)} %get-tuple-element.118.r_1_, bf16[768,1536]{1,0:T(8,128)(2,1)} %get-tuple-element.122.r_2_, ...), custom_call_target="tpu_custom_call" | custom-call | flops 16000000000 | bytes 16777216 | tf_op jit(solution)/shard_map/attend_back/pallas_call | solution.py:471
  269.9 8.1 %attend_back.6 = (f32[768,768]{1,0:T(8,128)}, bf16[768,768]{1,0:T(8,128)(2,1)}, bf16[768,768]{1,0:T(8,128)(2,1)}, bf16[768,768]{1,0:T(8,128)(2,1)}, f32[8,768]{1,0:T(8,128)}) custom-call(s32[1]{0:T(128)} %bitcast.t_ref.r_0_, bf16[768,1536]{1,0:T(8,128)(2,1)} %get-tuple-element.118.r_1_, bf16[768,1536]{1,0:T(8,128)(2,1)} %get-tuple-element.122.r_2_, ...), custom_call_target="tpu_custom_call" | custom-call | flops 16000000000 | bytes 16777216 | tf_op jit(solution)/shard_map/attend_back/pallas_call | solution.py:471
  280.9 24.2 %attend_back.7 = (bf16[768,768]{1,0:T(8,128)(2,1)}, bf16[768,768]{1,0:T(8,128)(2,1)}, bf16[768,768]{1,0:T(8,128)(2,1)}, f32[768,768]{1,0:T(8,128)}, f32[8,768]{1,0:T(8,128)}) custom-call(s32[1]{0:T(128)} %bitcast.t_ref.r_0_, bf16[768,1536]{1,0:T(8,128)(2,1)} %get-tuple-element.118.r_1_, bf16[768,1536]{1,0:T(8,128)(2,1)} %get-tuple-element.122.r_2_, ...), custom_call_target="tpu_custom_call" | custom-call | flops 16000000000 | bytes 16777216 | tf_op jit(solution)/shard_map/attend_back/pallas_call | solution.py:471
  308.6 12.7 %collective-permute-done.13.refs_2_ = bf16[4,2,96,768]{3,2,1,0:T(8,128)(2,1)} collective-permute-done((bf16[4,2,96,768]{3,2,1,0:T(8,128)(2,1)}, bf16[4,2,96,768]{3,2,1,0:T(8,128)(2,1)}, u32[]{:S(2)}, u32[]{:S(2)}) %collective-permute-start.13) | collective-permute-done | bytes 1179680 | tf_op jit(solution)/shard_map/ppermute | solution.py:1232
  325.9 33.6 %collective-permute-done.11.r_ref.refs_4_ = bf16[768,768]{1,0:T(8,128)(2,1)} collective-permute-done((bf16[768,768]{1,0:T(8,128)(2,1)S(1)}, bf16[768,768]{1,0:T(8,128)(2,1)}, u32[]{:S(2)}, u32[]{:S(2)}) %collective-permute-start.11) | collective-permute-done | bytes 1179680 | tf_op jit(solution)/shard_map/ppermute | solution.py:1248
  359.5 5.9 %attn_outer.2 = (bf16[4,96,1536]{2,1,0:T(8,128)(2,1)}, bf16[4,96,1536]{2,1,0:T(8,128)(2,1)}) custom-call(s32[1]{0:T(128)} %bitcast.14.core_ref, bf16[768,768]{1,0:T(8,128)(2,1)} %get-tuple-element.140.refs_0_, bf16[768,768]{1,0:T(8,128)(2,1)} %get-tuple-element.141.refs_1_, bf16[768,768]{1,0:T(8,128)(2,1)} %get-tuple-element.142.refs_2_.refs_0_, ...), custom_call_target="tpu_custom_call" | custom-call | flops 1811939328 | bytes 4718592 | tf_op jit(solution)/shard_map/attn_outer/pallas_call | solution.py:752
  365.4 14.2 %attn_outer.3 = (bf16[4,96,1536]{2,1,0:T(8,128)(2,1)}, bf16[4,96,1536]{2,1,0:T(8,128)(2,1)}) custom-call(s32[1]{0:T(128)} %bitcast.14.core_ref, bf16[768,768]{1,0:T(8,128)(2,1)} %get-tuple-element.142.refs_2_.refs_0_, bf16[768,768]{1,0:T(8,128)(2,1)} %get-tuple-element.164.refs_1_, bf16[768,768]{1,0:T(8,128)(2,1)} %get-tuple-element.165.refs_2_, ...), custom_call_target="tpu_custom_call" | custom-call | flops 7247757312 | bytes 14155776 | tf_op jit(solution)/shard_map/attn_outer/pallas_call | solution.py:752
  380.1 6.3 %collective-permute-start.30 = (bf16[2,96,768]{2,1,0:T(8,128)(2,1)}, bf16[2,96,768]{2,1,0:T(8,128)(2,1)S(1)}, u32[]{:S(2)}, u32[]{:S(2)}) collective-permute-start(bf16[2,96,768]{2,1,0:T(8,128)(2,1)} %get-tuple-element.189), channel_id=1, source_target_pairs={{0,1},{1,2},{2,3},{3,0},{4,5},{5,6},{6,7},{7,4},{8,9},{9,10},{10,1... | collective-permute-start | bytes 884744 | tf_op jit(solution)/shard_map/ppermute | solution.py:1229
  414.6 4.2 collective-permute-done.32.refs_3_
  433.2 7.7 %finish.1 = (bf16[768,768]{1,0:T(8,128)(2,1)}, bf16[768,768]{1,0:T(8,128)(2,1)}) custom-call(f32[768,768]{1,0:T(8,128)} %get-tuple-element.135.dx_ref, bf16[768,768]{1,0:T(8,128)(2,1)} %collective-permute-done.11.r_ref.refs_4_, bf16[768,768]{1,0:T(8,128)(2,1)} %sort_rows.2.x_ref.r_8_, f32[768,768]{1,0:T(8,128)} %get-tuple-element.136.mg_ref, ...), custom_call_target="tpu_custom_call" | custom-call | flops 1811939328 | bytes 9437184 | tf_op jit(solution)/shard_map/finish/pallas_call | solution.py:973
  (277 shorter events, 123.5 us)
Async XLA Ops:
  7.2 94.4 %all-gather.5.cloned.1.call-start = ((), (), s32[]{:S(2)}) async-start(), calls=%async_computation | async-start | bytes 6193152 | tf_op jit(solution)/shard_map/all_gather | solution.py:1175
  11.7 20.4 %collective-permute-start = (bf16[112,768]{1,0:T(8,128)(2,1)S(1)}, bf16[112,768]{1,0:T(8,128)(2,1)S(1)}, u32[]{:S(2)}, u32[]{:S(2)}) collective-permute-start(bf16[112,768]{1,0:T(8,128)(2,1)S(1)} %fusion.20.refs_0_), channel_id=1, source_target_pairs={{0,1},{1,2},{2,3},{3,0},{4,5},{5,6},{6,7},{7,4},{8,9},{9,10},{10,1... | collective-permute-start | bytes 516104 | tf_op jit(solution)/shard_map/ppermute | solution.py:1167
  14.8 17.3 %collective-permute-start.1 = (bf16[112,768]{1,0:T(8,128)(2,1)S(1)}, bf16[112,768]{1,0:T(8,128)(2,1)S(1)}, u32[]{:S(2)}, u32[]{:S(2)}) collective-permute-start(bf16[112,768]{1,0:T(8,128)(2,1)S(1)} %fusion.20.refs_0_), channel_id=1, source_target_pairs={{0,2},{1,3},{2,0},{3,1},{4,6},{5,7},{6,4},{7,5},{8,10},{9,11},{10,... | collective-permute-start | bytes 516104 | tf_op jit(solution)/shard_map/ppermute | solution.py:1167
  22.1 29.1 %collective-permute-start.3 = (bf16[768,768]{1,0:T(8,128)(2,1)}, bf16[768,768]{1,0:T(8,128)(2,1)S(1)}, u32[]{:S(2)}, u32[]{:S(2)}) collective-permute-start(bf16[768,768]{1,0:T(8,128)(2,1)} %sort_rows.2.x_ref.r_8_), channel_id=1, source_target_pairs={{0,1},{1,2},{2,3},{4,5},{5,6},{6,7},{8,9},{9,10},{10,11},{12,13},{... | collective-permute-start | bytes 3538952 | tf_op jit(solution)/shard_map/ppermute | solution.py:1141
  54.5 123.3 %all-gather.7.cloned.1.call-start = ((), (), s32[]{:S(2)}) async-start(), calls=%async_computation.1 | async-start | bytes 10616832 | tf_op jit(solution)/shard_map/all_gather | solution.py:1196
  57.3 52.2 %collective-permute-start.4 = (bf16[960,768]{1,0:T(8,128)(2,1)}, bf16[960,768]{1,0:T(8,128)(2,1)S(1)}, u32[]{:S(2)}, u32[]{:S(2)}) collective-permute-start(bf16[960,768]{1,0:T(8,128)(2,1)} %get-tuple-element.115.refs_0_), channel_id=1, source_target_pairs={{0,1},{1,2},{2,3},{3,0},{4,5},{5,6},{6,7},{7,4},{8,9},{9,10},{10,1... | collective-permute-start | bytes 4423688 | tf_op jit(solution)/shard_map/ppermute | solution.py:1182
  62.5 46.9 %collective-permute-start.6 = (bf16[192,768]{1,0:T(8,128)(2,1)}, bf16[192,768]{1,0:T(8,128)(2,1)S(1)}, u32[]{:S(2)}, u32[]{:S(2)}) collective-permute-start(bf16[192,768]{1,0:T(8,128)(2,1)} %get-tuple-element.121), channel_id=1, source_target_pairs={{0,2},{1,3},{2,0},{3,1},{4,6},{5,7},{6,4},{7,5},{8,10},{9,11},{10,... | collective-permute-start | bytes 884744 | tf_op jit(solution)/shard_map/ppermute | solution.py:1183
  64.4 44.9 %collective-permute-start.7 = (bf16[192,768]{1,0:T(8,128)(2,1)}, bf16[192,768]{1,0:T(8,128)(2,1)S(1)}, u32[]{:S(2)}, u32[]{:S(2)}) collective-permute-start(bf16[192,768]{1,0:T(8,128)(2,1)} %get-tuple-element.121), channel_id=1, source_target_pairs={{0,3},{1,0},{2,1},{3,2},{4,7},{5,4},{6,5},{7,6},{8,11},{9,8},{10,9... | collective-permute-start | bytes 884744 | tf_op jit(solution)/shard_map/ppermute | solution.py:1183
  114.8 30.0 %collective-permute-start.5 = (bf16[768,768]{1,0:T(8,128)(2,1)S(1)}, bf16[768,768]{1,0:T(8,128)(2,1)}, u32[]{:S(2)}, u32[]{:S(2)}) collective-permute-start(bf16[768,768]{1,0:T(8,128)(2,1)S(1)} %slice.79), channel_id=1, source_target_pairs={{2,3},{6,7},{10,11},{14,15},{18,19},{22,23},{26,27},{30,31}} | collective-permute-start | bytes 3538952 | tf_op jit(solution)/shard_map/ppermute | solution.py:1186
  241.5 22.5 %collective-permute-start.9 = (bf16[768,768]{1,0:T(8,128)(2,1)}, bf16[768,768]{1,0:T(8,128)(2,1)S(1)}, u32[]{:S(2)}, u32[]{:S(2)}) collective-permute-start(bf16[768,768]{1,0:T(8,128)(2,1)} %get-tuple-element.132), channel_id=1, source_target_pairs={{3,2},{7,6},{11,10},{15,14},{19,18},{23,22},{27,26},{31,30}} | collective-permute-start | bytes 3538952 | tf_op jit(solution)/shard_map/ppermute | solution.py:1248
  266.3 42.3 %collective-permute-start.12 = (bf16[4,2,96,768]{3,2,1,0:T(8,128)(2,1)}, bf16[4,2,96,768]{3,2,1,0:T(8,128)(2,1)}, u32[]{:S(2)}, u32[]{:S(2)}) collective-permute-start(bf16[4,2,96,768]{3,2,1,0:T(8,128)(2,1)} %get-tuple-element.144), channel_id=1, source_target_pairs={{0,8},{4,12},{8,0},{12,4},{16,24},{20,28},{24,16},{28,20},{1,9},{5... | collective-permute-start | bytes 3538952 | tf_op jit(solution)/shard_map/ppermute | solution.py:1232
  267.8 53.5 %collective-permute-start.13 = (bf16[4,2,96,768]{3,2,1,0:T(8,128)(2,1)}, bf16[4,2,96,768]{3,2,1,0:T(8,128)(2,1)}, u32[]{:S(2)}, u32[]{:S(2)}) collective-permute-start(bf16[4,2,96,768]{3,2,1,0:T(8,128)(2,1)} %get-tuple-element.145), channel_id=1, source_target_pairs={{0,16},{4,20},{8,24},{12,28},{16,0},{20,4},{24,8},{28,12},{1,17},{... | collective-permute-start | bytes 3538952 | tf_op jit(solution)/shard_map/ppermute | solution.py:1232
  268.4 52.9 %collective-permute-start.14 = (bf16[4,2,96,768]{3,2,1,0:T(8,128)(2,1)}, bf16[4,2,96,768]{3,2,1,0:T(8,128)(2,1)}, u32[]{:S(2)}, u32[]{:S(2)}) collective-permute-start(bf16[4,2,96,768]{3,2,1,0:T(8,128)(2,1)} %get-tuple-element.146), channel_id=1, source_target_pairs={{0,24},{4,28},{8,16},{12,20},{16,8},{20,12},{24,0},{28,4},{1,25},{... | collective-permute-start | bytes 3538952 | tf_op jit(solution)/shard_map/ppermute | solution.py:1232
  279.6 79.9 %collective-permute-start.11 = (bf16[768,768]{1,0:T(8,128)(2,1)S(1)}, bf16[768,768]{1,0:T(8,128)(2,1)}, u32[]{:S(2)}, u32[]{:S(2)}) collective-permute-start(bf16[768,768]{1,0:T(8,128)(2,1)S(1)} %add_convert_fusion.r_9_), channel_id=1, source_target_pairs={{1,0},{2,1},{3,2},{5,4},{6,5},{7,6},{9,8},{10,9},{11,10},{13,12},{... | collective-permute-start | bytes 3538952 | tf_op jit(solution)/shard_map/ppermute | solution.py:1248
  380.1 21.7 %collective-permute-start.30 = (bf16[2,96,768]{2,1,0:T(8,128)(2,1)}, bf16[2,96,768]{2,1,0:T(8,128)(2,1)S(1)}, u32[]{:S(2)}, u32[]{:S(2)}) collective-permute-start(bf16[2,96,768]{2,1,0:T(8,128)(2,1)} %get-tuple-element.189), channel_id=1, source_target_pairs={{0,1},{1,2},{2,3},{3,0},{4,5},{5,6},{6,7},{7,4},{8,9},{9,10},{10,1... | collective-permute-start | bytes 884744 | tf_op jit(solution)/shard_map/ppermute | solution.py:1229
  392.3 15.6 %collective-permute-start.25 = (bf16[96,1536]{1,0:T(8,128)(2,1)}, bf16[96,1536]{1,0:T(8,128)(2,1)S(1)}, u32[]{:S(2)}, u32[]{:S(2)}) collective-permute-start(bf16[96,1536]{1,0:T(8,128)(2,1)} %get-tuple-element.179), channel_id=1, source_target_pairs={{0,16},{4,20},{8,24},{12,28},{16,0},{20,4},{24,8},{28,12},{1,17},{... | collective-permute-start | bytes 884744 | tf_op jit(solution)/shard_map/ppermute | solution.py:1232
  393.9 15.1 %collective-permute-start.26 = (bf16[96,1536]{1,0:T(8,128)(2,1)}, bf16[96,1536]{1,0:T(8,128)(2,1)}, u32[]{:S(2)}, u32[]{:S(2)}) collective-permute-start(bf16[96,1536]{1,0:T(8,128)(2,1)} %get-tuple-element.180), channel_id=1, source_target_pairs={{0,24},{4,28},{8,16},{12,20},{16,8},{20,12},{24,0},{28,4},{1,25},{... | collective-permute-start | bytes 884744 | tf_op jit(solution)/shard_map/ppermute | solution.py:1232
  394.6 20.0 %collective-permute-start.31 = (bf16[2,96,768]{2,1,0:T(8,128)(2,1)}, bf16[2,96,768]{2,1,0:T(8,128)(2,1)S(1)}, u32[]{:S(2)}, u32[]{:S(2)}) collective-permute-start(bf16[2,96,768]{2,1,0:T(8,128)(2,1)} %get-tuple-element.190), channel_id=1, source_target_pairs={{0,2},{1,3},{2,0},{3,1},{4,6},{5,7},{6,4},{7,5},{8,10},{9,11},{10,... | collective-permute-start | bytes 884744 | tf_op jit(solution)/shard_map/ppermute | solution.py:1229
  401.9 21.8 %collective-permute-start.17 = (bf16[112,1536]{1,0:T(8,128)(2,1)}, bf16[112,1536]{1,0:T(8,128)(2,1)S(1)}, u32[]{:S(2)}, u32[]{:S(2)}) collective-permute-start(bf16[112,1536]{1,0:T(8,128)(2,1)} %get-tuple-element.157), channel_id=1, source_target_pairs={{0,8},{4,12},{8,0},{12,4},{16,24},{20,28},{24,16},{28,20},{1,9},{5... | collective-permute-start | bytes 1032200 | tf_op jit(solution)/shard_map/ppermute | solution.py:1232
  403.3 21.9 %collective-permute-start.18 = (bf16[112,1536]{1,0:T(8,128)(2,1)}, bf16[112,1536]{1,0:T(8,128)(2,1)S(1)}, u32[]{:S(2)}, u32[]{:S(2)}) collective-permute-start(bf16[112,1536]{1,0:T(8,128)(2,1)} %get-tuple-element.158), channel_id=1, source_target_pairs={{0,16},{4,20},{8,24},{12,28},{16,0},{20,4},{24,8},{28,12},{1,17},{... | collective-permute-start | bytes 1032200 | tf_op jit(solution)/shard_map/ppermute | solution.py:1232
  407.9 17.2 %collective-permute-start.19 = (bf16[112,1536]{1,0:T(8,128)(2,1)}, bf16[112,1536]{1,0:T(8,128)(2,1)S(1)}, u32[]{:S(2)}, u32[]{:S(2)}) collective-permute-start(bf16[112,1536]{1,0:T(8,128)(2,1)} %get-tuple-element.159), channel_id=1, source_target_pairs={{0,24},{4,28},{8,16},{12,20},{16,8},{20,12},{24,0},{28,4},{1,25},{... | collective-permute-start | bytes 1032200 | tf_op jit(solution)/shard_map/ppermute | solution.py:1232
  414.6 15.8 %collective-permute-start.27 = (bf16[96,384]{1,0:T(8,128)(2,1)}, bf16[96,384]{1,0:T(8,128)(2,1)S(1)}, u32[]{:S(2)}, u32[]{:S(2)}) collective-permute-start(bf16[96,384]{1,0:T(8,128)(2,1)} %get-tuple-element.182), channel_id=1, source_target_pairs={{0,1},{1,2},{2,3},{3,0},{4,5},{5,6},{6,7},{7,4},{8,9},{9,10},{10,1... | collective-permute-start | bytes 221192 | tf_op jit(solution)/shard_map/ppermute | solution.py:1229
  421.7 19.2 %collective-permute-start.28 = (bf16[96,384]{1,0:T(8,128)(2,1)S(1)}, bf16[96,384]{1,0:T(8,128)(2,1)S(1)}, u32[]{:S(2)}, u32[]{:S(2)}) collective-permute-start(bf16[96,384]{1,0:T(8,128)(2,1)S(1)} %copy-done.42), channel_id=1, source_target_pairs={{0,2},{1,3},{2,0},{3,1},{4,6},{5,7},{6,4},{7,5},{8,10},{9,11},{10,... | collective-permute-start | bytes 221192 | tf_op jit(solution)/shard_map/ppermute | solution.py:1229
  423.6 17.3 %collective-permute-start.29 = (bf16[96,384]{1,0:T(8,128)(2,1)S(1)}, bf16[96,384]{1,0:T(8,128)(2,1)S(1)}, u32[]{:S(2)}, u32[]{:S(2)}) collective-permute-start(bf16[96,384]{1,0:T(8,128)(2,1)S(1)} %copy-done.41), channel_id=1, source_target_pairs={{0,3},{1,0},{2,1},{3,2},{4,7},{5,4},{6,5},{7,6},{8,11},{9,8},{10,9... | collective-permute-start | bytes 221192 | tf_op jit(solution)/shard_map/ppermute | solution.py:1229
  (54 other events, 389.7 us)
Sparse Core Ops, SparseCore 0:
  54.6 46.9 all-gather.4
  113.2 64.6 all-gather.6
